TPU v7x, 256 devices: a whole 4x4x8 slice. The times are simulated.
256 devices in a mesh: gene: 4 (over x), sample: 16 (over y, z_lo, core), variant: 4 (over z_hi).
Axes of the slice: x: 4, y: 4, z: 8 (z_hi: 4, z_lo: 2; z = z_hi * 2 + z_lo), core: 2. Of those that a mesh axis runs over, the one named last changes fastest.
Arguments:
- expression: bfloat16 [65536, 4096], P('sample', 'gene'), may hold values from -6 to 6
- profile: float32 [4096, 7], P('gene'), may hold values from -0.25 to 0.25
- dosage: int32 [65536, 512], P('sample', 'variant'), may hold values from 0 to 2
- signature: int32 [500], replicated, may hold values from 0 to 4095, as said below
Outputs:
- interaction: float32 [3584, 4096], P(('variant', 'sample'), 'gene')
- proportions: float32 [65536, 7], P('sample')
Inputs may be any that keep to these rules, and one draw needn't show every extreme that they name: `signature`: distinct gene indices; gene 0 and gene 4096 - 1 are always among them.
All inputs are finite; a program needn't handle non-finite values.
Results may differ from a plain program's by a relative error of at most 0.0045.
Values sent between devices are 32-bit elements; how exact they have to be, the bound alone decides.
A program may use at most 128 MiB of HBM per device.

v0:
```python
import math

import jax
import jax.numpy as jnp
from jax import lax
from jax.sharding import PartitionSpec as P


def chol_solve(gram, rhs):
    factor = jnp.linalg.cholesky(gram)
    return jax.scipy.linalg.cho_solve((factor, True), rhs)


def local(expression, profile, dosage, signature):
    high = lax.Precision.HIGHEST
    s_dev, g_dev = expression.shape
    v_dev = dosage.shape[1]
    types = profile.shape[1]
    offset = lax.axis_index("gene") * g_dev
    local_ids = offset + lax.iota(jnp.int32, g_dev)
    member = jnp.any(local_ids[:, None] == signature[None, :], axis=1).astype(jnp.float32)
    masked = profile * member[:, None]
    gram = jnp.dot(masked.T, masked, precision=high)
    rhs = jnp.dot(masked.T, expression.T, precision=high, preferred_element_type=jnp.float32)
    gram_all, rhs_all = lax.psum((gram, rhs), "gene")
    props_t = chol_solve(gram_all, rhs_all)
    props = props_t.T
    pp_mat = jnp.dot(props_t, props, precision=high)
    py_mat = jnp.dot(props_t, expression, precision=high, preferred_element_type=jnp.float32)
    rounded = props.astype(jnp.bfloat16)
    design = (dosage.astype(jnp.bfloat16)[:, :, None] * rounded[:, None, :]).reshape(
        s_dev, v_dev * types
    )
    weights = (rounded.astype(jnp.float32)[:, :, None] * props[:, None, :]).reshape(
        s_dev, types * types
    )
    corr_t = jnp.dot(weights.T, dosage.astype(jnp.float32), precision=high)
    corr_t = corr_t.reshape(types, types, v_dev).transpose(1, 2, 0).reshape(types, v_dev * types)
    pp_all, py_all = lax.psum((pp_mat, py_mat), "sample")
    coef = chol_solve(pp_all, py_all)
    n_sample = lax.axis_size("sample")
    scale = jnp.float32(1.0 / math.sqrt(s_dev * n_sample))
    cross = lax.psum_scatter(
        lax.dot_general(
            design, expression, (((0,), (0,)), ((), ())), preferred_element_type=jnp.float32
        ),
        "sample",
        scatter_dimension=0,
        tiled=True,
    )
    corr_share = lax.psum_scatter(corr_t, "sample", scatter_dimension=1, tiled=True)
    interaction = (cross - jnp.dot(corr_share.T, coef, precision=high)) * scale
    return (interaction, props)


def solution(mesh):
    placed = (P("sample", "gene"), P("gene", None), P("sample", "variant"), P())
    return jax.shard_map(
        local,
        mesh=mesh,
        in_specs=placed,
        out_specs=(P(("variant", "sample"), "gene"), P("sample", None)),
        check_vma=False,
    )
```

profile of v0, /device:TPU:64, one launch (start us, length us, event | category | flops | bytes accessed | tf_op | source)
XLA Modules:
  0.0 178.5 jit_solution(5743142538719106987)
XLA Ops:
  7.2 1.2 compare_reduce_fusion
  8.4 10.7 %fusion.7 = f32[7,4096]{1,0:T(8,128)} fusion(bf16[4096,1024]{1,0:T(8,128)(2,1)} %param.5, f32[1024,7]{0,1:T(8,128)} %param.6, f32[1024]{0:T(1024)S(1)} %convert_element_type.20), kind=kOutput, calls=%fused_computation.9 | convolution fusion | flops 352328704 | bytes 8536064 | tf_op jit(solution)/shard_map/dot_general | solution.py:24
  19.3 10.5 %psum.28 = f32[7,7]{0,1:T(8,128)S(1)} all-reduce(f32[7,7]{0,1:T(8,128)S(1)} %fusion.9), channel_id=1, replica_groups=mesh['gene'=4,'sample'=16,'variant'=4] {'gene'}, use_global_device_ids=true, to_apply=%region_1.0 | all-reduce | flops 49 | bytes 392 | tf_op jit(solution)/shard_map/psum | solution.py:25
  29.9 0.6 cholesky.44
  30.6 0.6 compare_reduce_fusion.2
  31.2 0.6 fusion.13
  32.4 1.1 convert_element_type.19
  33.5 1.5 copy.29
  35.0 33.0 %all-reduce.4.cloned.1.call-done = f32[7,4096]{1,0:T(8,128)} async-done(((f32[7,4096]{1,0:T(8,128)}), f32[7,4096]{1,0:T(8,128)}) %all-reduce.4.cloned.1.call-update) | async-done | bytes 114704 | tf_op jit(solution)/shard_map/psum | solution.py:25
  68.1 1.2 fusion.19
  69.6 4.3 %broadcast_multiply_fusion = bf16[4096,128,7]{0,2,1:T(8,128)(2,1)} fusion(bf16[4096,7]{0,1:T(8,128)(2,1)S(1)} %get-tuple-element.7, bf16[4096,128]{0,1:T(8,128)(2,1)S(1)} %copy.29), kind=kLoop, calls=%fused_computation | loop fusion | flops 3670016 | bytes 8445952 | tf_op jit(solution)/shard_map/mul | solution.py:31
  73.9 9.5 %mul.57 = bf16[4096,896]{0,1:T(8,128)(2,1)} reshape(bf16[4096,128,7]{0,2,1:T(8,128)(2,1)} %broadcast_multiply_fusion) | data formatting | bytes 14680064 | tf_op jit(solution)/shard_map/mul | solution.py:31
  83.4 13.5 %fusion.28 = f32[896,1024]{1,0:T(8,128)} fusion(bf16[4096,896]{0,1:T(8,128)(2,1)} %mul.57, bf16[4096,1024]{1,0:T(8,128)(2,1)} %param.5), kind=kOutput, calls=%fused_computation.41 | convolution fusion | flops 7516192768 | bytes 19398656 | tf_op jit(solution)/shard_map/dot_general | solution.py:44
  97.0 0.6 dynamic-slice
  98.3 1.0 mul.61
  99.3 1.3 dot_general.29
  100.6 1.7 fusion.4
  103.1 5.7 %fusion.30 = f32[7,1024]{1,0:T(8,128)S(1)} fusion(f32[7,4096]{1,0:T(8,128)S(1)} %fusion.21, bf16[4096,1024]{1,0:T(8,128)(2,1)} %param.5), kind=kOutput, calls=%fused_computation.43 | convolution fusion | flops 352321536 | bytes 8531968 | tf_op jit(solution)/shard_map/dot_general | solution.py:29
  108.8 54.2 %all-reduce.1 = (f32[7,1024]{1,0:T(8,128)S(1)}, f32[7,7]{0,1:T(8,128)S(1)}, f32[7,896]{1,0:T(8,128)S(1)}) all-reduce(f32[7,1024]{1,0:T(8,128)S(1)} %fusion.30, f32[7,7]{0,1:T(8,128)S(1)} %fusion.29, f32[7,896]{1,0:T(8,128)S(1)} %reshape.48), channel_id=1, replica_groups=mesh['gene'=4,'sample'=16,'variant'=4] {'sample'}, use_global_device_ids=true, to_apply=%region_8.10 | all-reduce | flops 13489 | bytes 107912 | tf_op jit(solution)/shard_map/psum | solution.py:39
  163.1 0.6 cholesky.55
  163.7 0.6 compare_reduce_fusion.1
  164.4 0.6 fusion.14
  166.0 3.6 %reduce-scatter.3.cloned.1.call-done = f32[56,1024]{1,0:T(8,128)} async-done(((f32[896,1024]{1,0:T(8,128)}), f32[56,1024]{1,0:T(8,128)}) %reduce-scatter.3.cloned.1.call-update) | async-done | bytes 229392 | tf_op jit(solution)/shard_map/reduce_scatter | solution.py:43
  169.6 2.1 %fusion.3 = f32[56,1024]{1,0:T(8,128)} fusion(f32[56,1024]{1,0:T(8,128)} %reduce-scatter.3.cloned.1.call-done, f32[7,1024]{1,0:T(8,128)S(1)} %fusion.17, f32[7,896]{1,0:T(8,128)S(1)} %get-tuple-element.5, u32[]{:T(128)S(6)} %multiply.2), kind=kOutput, calls=%fused_computation.6 | convolution fusion | flops 4931584 | bytes 495620 | tf_op jit(solution)/shard_map/dot_general | solution.py:52
  (31 shorter events, 3.2 us)
Async XLA Ops:
  7.2 12.0 %copy-start.2 = (f32[1024,7]{0,1:T(8,128)S(1)}, f32[1024,7]{0,1:T(8,128)}, u32[]{:S(2)}) copy-start(f32[1024,7]{0,1:T(8,128)} %param.6) | copy-start | bytes 86020
  7.2 25.2 %copy-start = (s32[4096,128]{1,0:T(8,128)S(1)}, s32[4096,128]{1,0:T(8,128)}, u32[]{:S(2)}) copy-start(s32[4096,128]{1,0:T(8,128)} %param.7) | copy-start | bytes 6291460
  7.2 60.9 %all-reduce.4.cloned.1.call-start = ((), (), s32[]{:S(2)}) async-start(), calls=%async_computation.1 | async-start | bytes 262144 | tf_op jit(solution)/shard_map/psum | solution.py:25
  19.1 150.5 %reduce-scatter.3.cloned.1.call-start = ((), (), s32[]{:S(2)}) async-start(), calls=%async_computation.2 | async-start | bytes 3899392 | tf_op jit(solution)/shard_map/reduce_scatter | solution.py:43
  69.5 33.6 %copy-start.1 = (f32[7,4096]{1,0:T(8,128)}, f32[7,4096]{1,0:T(8,128)S(1)}, u32[]{:S(2)}) copy-start(f32[7,4096]{1,0:T(8,128)S(1)} %fusion.21) | copy-start | bytes 344068
  83.4 13.6 %copy-start.3 = (u32[256]{0:T(256)S(1)}, u32[256]{0:T(256)}, u32[]{:S(2)}) copy-start(u32[256]{0:T(256)} %constant.65) | copy-start | bytes 3076
Sparse Core Ops, SparseCore 0:
  19.2 48.7 all-reduce.3
  97.1 72.4 reduce-scatter.2
where the time goes:
time: 180 us; the launch traced here: 179 us
  blocking collectives  64.7 us (36%)
  waiting for transfers between devices  36.7 us (20%)
  matrix products  36 us (20%)
  between operations  14.8 us (8%)
  local copies, waits for them, and re-layouts  14.6 us (8%)
  other arithmetic  11.7 us (6%)
    psum x1, blocking collectives, local(): pp_all, py_all = lax.psum((pp_mat, py_mat), 'sample')  54.2 us
    psum x1, waiting for transfers between devices, local(): gram_all, rhs_all = lax.psum((gram, rhs), 'gene')  33 us
    dot_general x1, matrix products, local(): lax.dot_general(design, expression, (((0,), (0,)), ((), ())), preferred_e...  13.5 us
    dot_general x1, matrix products, local(): jnp.dot(masked.T, expression.T, precision=high, preferred_element_type=jn...  10.7 us
    psum x1, blocking collectives, local(): gram_all, rhs_all = lax.psum((gram, rhs), 'gene')  10.5 us
    mul x1, local copies, waits for them, and re-layouts, local(): dosage.astype(jnp.bfloat16)[:, :, None] * rounded[:, None, :]  9.5 us
    dot_general x1, matrix products, local(): jnp.dot(props_t, expression, precision=high, preferred_element_type=jnp.f...  5.69 us
    mul x1, other arithmetic, local(): dosage.astype(jnp.bfloat16)[:, :, None] * rounded[:, None, :]  4.3 us
  transfers between devices with their start and end apart: 2, of which 2 were waited for; matrix products, arithmetic and copies ran while one was open for 11% of the time, Pallas kernels for 0%

commit v1 on v0

v1 whole, which is shorter than its diff:
```python
import functools
import math

import jax
import jax.numpy as jnp
from jax import lax
from jax.experimental import pallas as pl
from jax.experimental.pallas import tpu as pltpu
from jax.sharding import PartitionSpec as P

MESH = pl.DeviceIdType.MESH
HIGH = lax.Precision.HIGHEST
F32, BF16 = jnp.float32, jnp.bfloat16
NT = (((1,), (1,)), ((), ()))
N_GENE = 4
N_SAMPLE = 16
N_CHUNK = 4
PARTS = ((0, 2, "abz"), (2, 4, "zab"), (4, 7, "bza"))


def ldl(gram):
    row = lax.broadcasted_iota(jnp.int32, (8, 8), 0)
    col = lax.broadcasted_iota(jnp.int32, (8, 8), 1)
    eye = (row == col).astype(F32)
    a = jnp.where((row == 7) | (col == 7), eye, gram)
    inv, inv_t = eye, eye
    for j in range(6):
        piv = a[j : j + 1, j : j + 1]
        f_col = jnp.where(row[:, :1] > j, a[:, j : j + 1] / piv, 0.0)
        f_row = jnp.where(col[:1, :] > j, a[j : j + 1, :] / piv, 0.0)
        inv = inv - f_col * inv[j : j + 1, :]
        inv_t = inv_t - inv_t[:, j : j + 1] * f_row
        a = a - f_col * a[j : j + 1, :]
    diag = jnp.sum(a * eye, axis=1, keepdims=True)
    return inv, inv_t, diag


def solve(factor, rhs):
    inv, inv_t, diag = factor
    mid = inv[:, 0:1] * rhs[0:1, :]
    for j in range(1, 7):
        mid = mid + inv[:, j : j + 1] * rhs[j : j + 1, :]
    mid = mid / diag
    out = inv_t[:, 0:1] * mid[0:1, :]
    for j in range(1, 7):
        out = out + inv_t[:, j : j + 1] * mid[j : j + 1, :]
    return out


def kernel(
    scale,
    sig_ref, prof_ref, expr_hbm, dos_hbm,
    inter_ref, props_ref,
    e_v, d_v, d_t, des, w_hi, w_lo, sig_sc, m_sc, acc, rc, r1, r2, r3, facc,
    pbuf, rsnd, rrcv, gsnd, grcv, corr_sc, pp_sc, tsrc, trcv, tbuf, mix,
    e_sem, d_sem, g_s, g_r, x_s, x_r, p_s, p_r, c_s, c_r, h_s, h_r, t_s, t_r, u_s, u_r,
):
    s_dev, g_dev = e_v.shape
    quarter = s_dev // N_GENE
    half = quarter // 2
    n_cols = g_dev // N_CHUNK
    types = 7
    g = lax.axis_index("gene")
    s = lax.axis_index("sample")
    y, z, c = s // 4, (s // 2) % 2, s % 2
    b = y // 2
    a = (y + b) % 2
    place = {"a": a, "b": b, "z": z}
    other = {
        "a": (2 * b + (1 - a + b) % 2) * 4 + z * 2 + c,
        "b": (2 * (1 - b) + (a + 1 - b) % 2) * 4 + z * 2 + c,
        "z": s + 2 - 4 * z,
    }
    core = s + 1 - 2 * c

    def gene_of(d):
        return {"gene": (g + d) % N_GENE}

    def sample_of(d):
        return {"sample": (s + d) % N_SAMPLE}

    def load(d, h):
        rows = pl.ds(pl.multiple_of(((g + d) % N_GENE) * quarter + h * half, half), half)
        return pltpu.make_async_copy(expr_hbm.at[rows, :], e_v.at[rows, :], e_sem.at[d, h])

    def remote(src, dst, send, recv, device):
        return pltpu.make_async_remote_copy(
            src_ref=src, dst_ref=dst, send_sem=send, recv_sem=recv, device_id=device, device_id_type=MESH
        )

    order = (2, 1, 3, 0)
    for d in order:
        for h in range(2):
            load(d, h).start()
    dos_copy = pltpu.make_async_copy(dos_hbm, d_v, d_sem)
    dos_copy.start()

    barrier = pltpu.get_barrier_semaphore()
    for d in range(1, N_GENE):
        pl.semaphore_signal(barrier, inc=1, device_id=gene_of(d), device_id_type=MESH)
    for d in range(1, N_SAMPLE):
        pl.semaphore_signal(barrier, inc=1, device_id=sample_of(d), device_id_type=MESH)

    n_sig = sig_ref.shape[1]
    sig_sc[...] = jnp.full(sig_sc.shape, -1, jnp.int32)
    sig_sc[0:1, 0:n_sig] = sig_ref[...]
    cols = []
    for t in range(sig_sc.shape[1] // 128):
        line = sig_sc[0:1, 128 * t : 128 * t + 128].astype(F32)
        cols.append(jnp.transpose(jnp.broadcast_to(line, (128, 128))))
    lane = lax.broadcasted_iota(jnp.int32, (128, 128), 1) + g * g_dev
    m_sc[...] = jnp.zeros(m_sc.shape, F32)
    for t in range(g_dev // 128):
        ids = (lane + 128 * t).astype(F32)
        hit = jnp.zeros((128, 128), F32)
        for column in cols:
            hit = jnp.where(column == ids, 1.0, hit)
        member = jnp.max(hit, axis=0, keepdims=True)
        m_sc[0:types, 128 * t : 128 * t + 128] = prof_ref[:, 128 * t : 128 * t + 128] * member
    masked = m_sc[...]
    gsnd[...] = jnp.zeros(gsnd.shape, F32)
    gsnd[:, 0:8] = lax.dot_general(masked, masked, NT, precision=HIGH, preferred_element_type=F32)
    top = masked.astype(BF16).astype(F32)
    rest = masked - top
    mid = rest.astype(BF16).astype(F32)
    m3 = jnp.concatenate([top, mid, rest - mid], axis=0).astype(BF16)

    pl.semaphore_wait(barrier, N_GENE - 1 + N_SAMPLE - 1)

    def gram_copy(d):
        return remote(gsnd, grcv.at[d - 1], g_s.at[d - 1], g_r.at[d - 1], gene_of(d))

    def rhs_copy(d):
        return remote(rsnd.at[d], rrcv.at[d - 1], x_s.at[d - 1], x_r.at[d - 1], gene_of(d))

    for d in range(1, N_GENE):
        gram_copy(d).start()
    for d in order:
        for h in range(2):
            load(d, h).wait()
            rows = pl.ds(pl.multiple_of(((g + d) % N_GENE) * quarter + h * half, half), half)
            part = lax.dot_general(m3, e_v[rows, :], NT, preferred_element_type=F32)
            rsnd[d, :, h * half : (h + 1) * half] = part[0:8] + part[8:16] + part[16:24]
        if d:
            rhs_copy(d).start()

    dos_copy.wait()

    def turn(i, carry):
        rows = pl.ds(pl.multiple_of(i * 128, 128), 128)
        d_t[:, rows] = jnp.transpose(d_v[rows, :].astype(F32)).astype(BF16)
        return carry

    lax.fori_loop(0, s_dev // 128, turn, 0)
    gram = gsnd[:, 0:8]
    for d in range(1, N_GENE):
        gram_copy(d).wait_recv()
        gram = gram + grcv[d - 1, :, 0:8]
    factor = ldl(gram)
    rhs = rsnd[0]
    for d in (1, 3, 2):
        rhs_copy(d).wait_recv()
        rhs = rhs + rrcv[d - 1]
    pbuf[g] = solve(factor, rhs)

    def props_copy(d):
        return remote(pbuf.at[g], pbuf.at[g], p_s.at[d - 1], p_r.at[d - 1], gene_of(d))

    for d in (2, 1, 3):
        props_copy(d).start()

    corr_sc[...] = jnp.zeros(corr_sc.shape, F32)
    pp_sc[...] = jnp.zeros(pp_sc.shape, F32)
    for d in (0, 1, 3, 2):
        if d:
            props_copy(d).wait_recv()
        q = (g + N_GENE - d) % N_GENE
        span = pl.ds(pl.multiple_of(q * quarter, quarter), quarter)
        props = pbuf[q]
        props_ref[:, span] = props[0:types]
        top = props.astype(BF16).astype(F32)
        des[896:912, span] = jnp.concatenate([top, props - top], axis=0).astype(BF16)
        highs, lows = [], []
        for k in range(types):
            wide = jnp.broadcast_to(top[k : k + 1, :], (16, quarter)).astype(BF16)
            for bb in range(2):
                for aa in range(2):
                    for zz in range(2):
                        source = ((2 * bb + (aa + bb) % 2) * 2 + zz) * 16
                        target = (((bb * 2 + aa) * 2 + zz) * types + k) * 16
                        des[target : target + 16, span] = d_t[source : source + 16, span] * wide
            weight = jnp.broadcast_to(top[k : k + 1, :], (8, quarter)) * props
            high = weight.astype(BF16).astype(F32)
            highs.append(high)
            lows.append(weight - high)
        w_hi[...] = jnp.concatenate(highs, axis=0).astype(BF16)
        w_lo[...] = jnp.concatenate(lows, axis=0).astype(BF16)
        turned = d_t[:, span]
        corr_sc[:, 0:56] += lax.dot_general(
            turned, w_hi[...], NT, preferred_element_type=F32
        ) + lax.dot_general(turned, w_lo[...], NT, preferred_element_type=F32)
        pp_sc[:, 0:8] += lax.dot_general(props, props, NT, precision=HIGH, preferred_element_type=F32)

    def core_copy(n):
        return remote(
            acc.at[n, :, :, :, :, 1 - c], rc.at[n], c_s.at[n], c_r.at[n], {"sample": core}
        )

    def block(n, ks, fixed):
        at = tuple(fixed.get(axis, slice(None)) for axis in "baz")
        return (n,) + at + (ks, c)

    def halving(n, part, step):
        lo, hi, axes = PARTS[part]
        ks = slice(lo, hi)
        kept = {axis: place[axis] for axis in axes[:step]}
        axis = axes[step]
        landing = ((r1, r2, r3)[step])[part].at[n]
        copy = remote(
            acc.at[block(n, ks, {**kept, axis: 1 - place[axis]})],
            landing,
            h_s.at[n, part, step],
            h_r.at[n, part, step],
            {"sample": other[axis]},
        )
        return copy, block(n, ks, {**kept, axis: place[axis]}), landing

    def tile_copy(d):
        return remote(tsrc.at[(s + d) % N_SAMPLE], trcv.at[d - 1], t_s.at[d - 1], t_r.at[d - 1], sample_of(d))

    def spread_copy(d):
        return remote(tbuf.at[s], tbuf.at[s], u_s.at[d - 1], u_r.at[d - 1], sample_of(d))

    def stage(t, carry):
        @pl.when(t < N_CHUNK)
        def _():
            columns = pl.ds(pl.multiple_of(t * n_cols, n_cols), n_cols)
            shape = acc.shape[1:]

            def term(q):
                span = pl.ds(pl.multiple_of(q * quarter, quarter), quarter)
                return jnp.dot(des[:, span], e_v[span, columns], preferred_element_type=F32)

            def put(value, first):
                body, tail = value[0:896].reshape(shape), value[896:904] + value[904:912]
                for i in range(n_cols // 128):
                    piece = tail[:, 128 * i : 128 * i + 128]
                    at = t * (n_cols // 128) + i
                    tsrc[at, 1] = piece if first else tsrc[at, 1] + piece
                acc[t] = body if first else acc[t] + body

            put(term(0), True)

            def more(q, carry):
                put(term(q), False)
                return carry

            lax.fori_loop(1, N_GENE, more, 0)
            core_copy(t).start()

        @pl.when((t >= 1) & (t < N_CHUNK + 1))
        def _():
            n = t - 1
            core_copy(n).wait_recv()
            acc[n, :, :, :, :, c] += rc[n]
            for part in range(3):
                halving(n, part, 0)[0].start()

        for step in range(3):
            @pl.when((t >= 2 + step) & (t < N_CHUNK + 2 + step))
            def _(step=step):
                n = t - 2 - step
                for part in range(3):
                    copy, kept, landing = halving(n, part, step)
                    copy.wait_recv()
                    if step < 2:
                        acc[kept] += landing[...]
                        halving(n, part, step + 1)[0].start()
                    else:
                        lo, hi, _ = PARTS[part]
                        at = pl.ds(pl.multiple_of(n * n_cols, n_cols), n_cols)
                        facc[lo:hi, :, at] = acc[kept] + landing[...]

        @pl.when(t == N_CHUNK - 1)
        def _():
            for i in range(N_SAMPLE):
                tsrc[i, 0] = corr_sc[8 * i : 8 * i + 8, :]
            tsrc[g_dev // 128, 1] = pp_sc[...]
            for i in range(g_dev // 128 + 1, N_SAMPLE):
                tsrc[i, 1] = jnp.zeros((8, 128), F32)

            def send(d, carry):
                tile_copy(d).start()
                return carry

            lax.fori_loop(1, N_SAMPLE, send, 0)

        @pl.when(t == N_CHUNK + 1)
        def _():
            def take(d, carry):
                tile_copy(d).wait_recv()
                return carry + trcv[d - 1]

            total = lax.fori_loop(1, N_SAMPLE, take, tsrc[s])
            corr_sc[0:8, :] = total[0]
            tbuf[s] = total[1]

            def send(d, carry):
                spread_copy(d).start()
                return carry

            lax.fori_loop(1, N_SAMPLE, send, 0)

        return carry

    lax.fori_loop(0, N_CHUNK + 4, stage, 0)

    def gather(d, carry):
        spread_copy(d).wait_recv()
        return carry

    lax.fori_loop(1, N_SAMPLE, gather, 0)
    n_tiles = g_dev // 128
    py = jnp.concatenate([tbuf[i] for i in range(n_tiles)], axis=1)
    coef = solve(ldl(tbuf[n_tiles, :, 0:8]), py)
    corr = corr_sc[0:8, :]
    for k in range(types):
        value = facc[k]
        for j in range(types):
            value = value - corr[:, 8 * k + j : 8 * k + j + 1] * coef[j : j + 1, :]
        value = value * scale
        for i in range(n_tiles):
            mix[i, pl.ds(k, 8, stride=types), :] = value[:, 128 * i : 128 * i + 128]
    for i in range(n_tiles):
        inter_ref[:, 128 * i : 128 * i + 128] = mix[i]

    for d in range(1, N_GENE):
        gram_copy(d).wait_send()
        rhs_copy(d).wait_send()
        props_copy(d).wait_send()

    def drain(n, carry):
        core_copy(n).wait_send()
        for part in range(3):
            for step in range(3):
                halving(n, part, step)[0].wait_send()
        return carry

    lax.fori_loop(0, N_CHUNK, drain, 0)

    def drain_tiles(d, carry):
        tile_copy(d).wait_send()
        spread_copy(d).wait_send()
        return carry

    lax.fori_loop(1, N_SAMPLE, drain_tiles, 0)


def local(expression, profile, dosage, signature):
    s_dev, g_dev = expression.shape
    v_dev = dosage.shape[1]
    types = profile.shape[1]
    quarter, n_cols = s_dev // N_GENE, g_dev // N_CHUNK
    scale = 1.0 / math.sqrt(s_dev * N_SAMPLE)
    sig_cols = -(-signature.shape[0] // 128) * 128
    sizes = [hi - lo for lo, hi, _ in PARTS]
    vmem, dma = pltpu.VMEM, pltpu.SemaphoreType.DMA
    inter, props_t = pl.pallas_call(
        functools.partial(kernel, scale),
        out_shape=(
            jax.ShapeDtypeStruct((v_dev * types // N_SAMPLE, g_dev), F32),
            jax.ShapeDtypeStruct((types, s_dev), F32),
        ),
        in_specs=[
            pl.BlockSpec(memory_space=pltpu.VMEM),
            pl.BlockSpec(memory_space=pltpu.VMEM),
            pl.BlockSpec(memory_space=pl.ANY),
            pl.BlockSpec(memory_space=pl.ANY),
        ],
        out_specs=(pl.BlockSpec(memory_space=pltpu.VMEM), pl.BlockSpec(memory_space=pltpu.VMEM)),
        scratch_shapes=[
            vmem((s_dev, g_dev), BF16),
            vmem((s_dev, v_dev), jnp.int32),
            vmem((v_dev, s_dev), BF16),
            vmem((v_dev * types + 16, s_dev), BF16),
            vmem((8 * types, quarter), BF16),
            vmem((8 * types, quarter), BF16),
            vmem((1, sig_cols), jnp.int32),
            vmem((8, g_dev), F32),
            vmem((N_CHUNK, 2, 2, 2, types, 2, 8, n_cols), F32),
            vmem((N_CHUNK, 2, 2, 2, types, 8, n_cols), F32),
            [vmem((N_CHUNK, 2, 2, k, 8, n_cols), F32) for k in sizes],
            [vmem((N_CHUNK, 2, k, 8, n_cols), F32) for k in sizes],
            [vmem((N_CHUNK, k, 8, n_cols), F32) for k in sizes],
            vmem((types, 8, g_dev), F32),
            vmem((N_GENE, 8, quarter), F32),
            vmem((N_GENE, 8, quarter), F32),
            vmem((N_GENE - 1, 8, quarter), F32),
            vmem((8, 128), F32),
            vmem((N_GENE - 1, 8, 128), F32),
            vmem((v_dev, 128), F32),
            vmem((8, 128), F32),
            vmem((N_SAMPLE, 2, 8, 128), F32),
            vmem((N_SAMPLE - 1, 2, 8, 128), F32),
            vmem((N_SAMPLE, 8, 128), F32),
            vmem((g_dev // 128, 8 * types, 128), F32),
            dma((N_GENE, 2)),
            dma,
            dma((N_GENE - 1,)),
            dma((N_GENE - 1,)),
            dma((N_GENE - 1,)),
            dma((N_GENE - 1,)),
            dma((N_GENE - 1,)),
            dma((N_GENE - 1,)),
            dma((N_CHUNK,)),
            dma((N_CHUNK,)),
            dma((N_CHUNK, 3, 3)),
            dma((N_CHUNK, 3, 3)),
            dma((N_SAMPLE - 1,)),
            dma((N_SAMPLE - 1,)),
            dma((N_SAMPLE - 1,)),
            dma((N_SAMPLE - 1,)),
        ],
        compiler_params=pltpu.CompilerParams(
            collective_id=0, has_side_effects=True, vmem_limit_bytes=60 * 1024 * 1024
        ),
        name="eqtl",
    )(signature.reshape(1, -1), profile.T, expression, dosage)
    return inter, props_t.T


def solution(mesh):
    placed = (P("sample", "gene"), P("gene", None), P("sample", "variant"), P())
    return jax.shard_map(
        local,
        mesh=mesh,
        in_specs=placed,
        out_specs=(P(("variant", "sample"), "gene"), P("sample", None)),
        check_vma=False,
    )
```

time: 180 us -> 52.9 us (0.29)
  blocking collectives: 64.7 us -> 0 us
  Pallas kernels: 0 us -> 48 us
  waiting for transfers between devices: 36.7 us -> 0 us
  matrix products: 36 us -> 0 us
  between operations: 14.8 us -> 0.64 us
  other arithmetic: 11.7 us -> 0 us
  local copies, waits for them, and re-layouts: 14.6 us -> 3.21 us
    psum x2 -> x0, blocking collectives: 64.7 us -> none  [the longest x1 54.2 us: local(): pp_all, py_all = lax.psum((pp_mat, py_mat), 'sample')]
    pallas_call x0 -> x1, Pallas kernels: none -> 48 us  [local(): pl.pallas_call(functools.partial(kernel, scale), out_shape=(jax.ShapeDtyp...]
    dot_general x7 -> x0, matrix products: 34.1 us -> none  [the longest x1 13.5 us: local(): lax.dot_general(design, expression, (((0,), (0,)), ((), ())), preferred_e...]
    psum x1 -> x0, waiting for transfers between devices: 33 us -> none  [local(): gram_all, rhs_all = lax.psum((gram, rhs), 'gene')]
    mul x2 -> x0, local copies, waits for them, and re-layouts: 10.5 us -> none  [the longest x1 9.5 us: local(): dosage.astype(jnp.bfloat16)[:, :, None] * rounded[:, None, :]]
    another operation x10 -> x0, other arithmetic: 5 us -> none  [the longest x6 2.6 us: chol_solve(): factor = jnp.linalg.cholesky(gram)]
    mul x2 -> x0, other arithmetic: 4.37 us -> none  [the longest x1 4.3 us: local(): dosage.astype(jnp.bfloat16)[:, :, None] * rounded[:, None, :]]
    reduce_scatter x1 -> x0, waiting for transfers between devices: 3.59 us -> none  [local(): lax.psum_scatter(lax.dot_general(design, expression, (((0,), (0,)), ((),...]
  transfers between devices with their start and end apart: 2 -> 0, of which waited for: 2 -> 0; matrix products, arithmetic and copies ran while one was open for 11% -> 0% of each run, Pallas kernels for 0% -> 0%
where the time goes in v1:
time: 52.9 us; the launch traced here: 51.9 us
  Pallas kernels  48 us (91%)
  local copies, waits for them, and re-layouts  3.21 us (6%)
  between operations  0.64 us (1%)
    pallas_call x1, Pallas kernels, local(): pl.pallas_call(functools.partial(kernel, scale), out_shape=(jax.ShapeDtyp...  48 us
    unnamed x2, local copies, waits for them, and re-layouts  3.21 us

profile of v1, /device:TPU:64, one launch (start us, length us, event | category | flops | bytes accessed | tf_op | source)
XLA Modules:
  0.0 51.9 jit_solution(718345904602634505)
XLA Ops:
  0.6 48.0 %eqtl.1 = (f32[56,1024]{1,0:T(8,128)}, f32[7,4096]{1,0:T(8,128)}) custom-call(s32[1,500]{1,0:T(1,128)} %bitcast.5, f32[7,1024]{1,0:T(8,128)} %bitcast.4, bf16[4096,1024]{1,0:T(8,128)(2,1)} %expr_hbm.1, s32[4096,128]{1,0:T(8,128)} %dos_hbm.1), custom_call_target="tpu_custom_call" | custom-call | tf_op jit(solution)/shard_map/eqtl/pallas_call | solution.py:368
  48.7 1.6 %copy.8 = f32[56,1024]{1,0:T(8,128)} copy(f32[56,1024]{1,0:T(8,128)} %get-tuple-element.8) | data formatting | bytes 458752
  50.3 1.6 %copy.9 = f32[4096,7]{0,1:T(8,128)} copy(f32[4096,7]{0,1:T(8,128)} %bitcast.3) | data formatting | bytes 229376

commit v2 on v1

v2 whole, which is shorter than its diff:
```python
import functools
import math

import jax
import jax.numpy as jnp
from jax import lax
from jax.experimental import pallas as pl
from jax.experimental.pallas import tpu as pltpu
from jax.sharding import PartitionSpec as P

MESH = pl.DeviceIdType.MESH
HIGH = lax.Precision.HIGHEST
F32, BF16 = jnp.float32, jnp.bfloat16
NT = (((1,), (1,)), ((), ()))
N_GENE = 4
N_SAMPLE = 16
N_CHUNK = 4
VMEM_BYTES = 62_000_000
PARTS = ((0, 2), (2, 4), (4, 7))
ORDERS = ("abz", "zab", "bza")


def ldl(gram):
    row = lax.broadcasted_iota(jnp.int32, (8, 8), 0)
    col = lax.broadcasted_iota(jnp.int32, (8, 8), 1)
    eye = (row == col).astype(F32)
    a = jnp.where((row == 7) | (col == 7), eye, gram)
    inv, inv_t = eye, eye
    for j in range(6):
        piv = a[j : j + 1, j : j + 1]
        f_col = jnp.where(row[:, :1] > j, a[:, j : j + 1] / piv, 0.0)
        f_row = jnp.where(col[:1, :] > j, a[j : j + 1, :] / piv, 0.0)
        inv = inv - f_col * inv[j : j + 1, :]
        inv_t = inv_t - inv_t[:, j : j + 1] * f_row
        a = a - f_col * a[j : j + 1, :]
    diag = jnp.sum(a * eye, axis=1, keepdims=True)
    return inv, inv_t, diag


def solve(factor, rhs):
    inv, inv_t, diag = factor
    mid = inv[:, 0:1] * rhs[0:1, :]
    for j in range(1, 7):
        mid = mid + inv[:, j : j + 1] * rhs[j : j + 1, :]
    mid = mid / diag
    out = inv_t[:, 0:1] * mid[0:1, :]
    for j in range(1, 7):
        out = out + inv_t[:, j : j + 1] * mid[j : j + 1, :]
    return out


def kernel(
    scale,
    sig_ref, prof_ref, expr_hbm, dos_hbm,
    inter_ref, props_ref,
    e_v, d_v, d_t, des, sig_sc, m_sc, acc, rc, r1, r2, r3,
    pbuf, rsnd, rrcv, gsnd, grcv, corr_sc, pp_sc, py_sc, fac_sc, tsrc, trcv, tbuf, mix,
    e_sem, d_sem, g_s, g_r, x_s, x_r, p_s, p_r, c_s, c_r, h_s, h_r, t_s, t_r, u_s, u_r,
):
    s_dev, g_dev = e_v.shape
    quarter = s_dev // N_GENE
    half = quarter // 2
    n_cols = g_dev // N_CHUNK
    n_tiles = g_dev // 128
    per_chunk = n_cols // 128
    types = 7
    g = lax.axis_index("gene")
    s = lax.axis_index("sample")
    y, z, c = s // 4, (s // 2) % 2, s % 2
    b = y // 2
    a = (y + b) % 2
    place = {"a": a, "b": b, "z": z}
    other = {
        "a": (2 * b + (1 - a + b) % 2) * 4 + z * 2 + c,
        "b": (2 * (1 - b) + (a + 1 - b) % 2) * 4 + z * 2 + c,
        "z": s + 2 - 4 * z,
    }
    core = s + 1 - 2 * c

    def gene_of(d):
        return {"gene": (g + d) % N_GENE}

    def sample_of(d):
        return {"sample": (s + d) % N_SAMPLE}

    def rows_of(d, h):
        return pl.ds(pl.multiple_of(((g + d) % N_GENE) * quarter + h * half, half), half)

    def load(d, h):
        return pltpu.make_async_copy(expr_hbm.at[rows_of(d, h), :], e_v.at[rows_of(d, h), :], e_sem.at[d, h])

    def remote(src, dst, send, recv, device):
        return pltpu.make_async_remote_copy(
            src_ref=src, dst_ref=dst, send_sem=send, recv_sem=recv, device_id=device, device_id_type=MESH
        )

    for d in (3, 2, 1, 0):
        for h in range(2):
            load(d, h).start()
    dos_copy = pltpu.make_async_copy(dos_hbm, d_v, d_sem)
    dos_copy.start()

    barrier = pltpu.get_barrier_semaphore()
    for d in range(1, N_GENE):
        pl.semaphore_signal(barrier, inc=1, device_id=gene_of(d), device_id_type=MESH)
    for d in range(1, N_SAMPLE):
        pl.semaphore_signal(barrier, inc=1, device_id=sample_of(d), device_id_type=MESH)

    n_sig = sig_ref.shape[1]
    sig_sc[...] = jnp.full(sig_sc.shape, -1, jnp.int32)
    sig_sc[0:1, 0:n_sig] = sig_ref[...]
    cols = []
    for t in range(sig_sc.shape[1] // 128):
        line = sig_sc[0:1, 128 * t : 128 * t + 128].astype(F32)
        cols.append(jnp.transpose(jnp.broadcast_to(line, (128, 128))))
    lane = lax.broadcasted_iota(jnp.int32, (128, 128), 1) + g * g_dev
    m_sc[...] = jnp.zeros(m_sc.shape, F32)
    for t in range(n_tiles):
        ids = (lane + 128 * t).astype(F32)
        hit = jnp.zeros((128, 128), F32)
        for column in cols:
            hit = jnp.where(column == ids, 1.0, hit)
        member = jnp.max(hit, axis=0, keepdims=True)
        m_sc[0:types, 128 * t : 128 * t + 128] = prof_ref[:, 128 * t : 128 * t + 128] * member
    masked = m_sc[...]
    gsnd[...] = jnp.zeros(gsnd.shape, F32)
    gsnd[:, 0:8] = lax.dot_general(masked, masked, NT, precision=HIGH, preferred_element_type=F32)
    top = masked.astype(BF16).astype(F32)
    rest = masked - top
    mid = rest.astype(BF16).astype(F32)
    m3 = jnp.concatenate([top, mid, rest - mid], axis=0).astype(BF16)

    def gram_copy(d):
        return remote(gsnd, grcv.at[d - 1], g_s.at[d - 1], g_r.at[d - 1], gene_of(d))

    def rhs_copy(d):
        return remote(rsnd.at[d], rrcv.at[d - 1], x_s.at[d - 1], x_r.at[d - 1], gene_of(d))

    def rhs_half(i, carry):
        d, h = N_GENE - 1 - i // 2, i % 2
        load(d, h).wait()
        part = lax.dot_general(m3, e_v[rows_of(d, h), :], NT, preferred_element_type=F32)
        rsnd[d, :, pl.ds(pl.multiple_of(h * half, half), half)] = part[0:8] + part[8:16] + part[16:24]

        @pl.when(i == 1)
        def _():
            pl.semaphore_wait(barrier, N_GENE - 1 + N_SAMPLE - 1)
            for peer in range(1, N_GENE):
                gram_copy(peer).start()

        @pl.when((h == 1) & (d > 0))
        def _():
            rhs_copy(d).start()

        return carry

    lax.fori_loop(0, 2 * N_GENE, rhs_half, 0)

    dos_copy.wait()
    for i in range(s_dev // 128):
        piece = d_v[128 * i : 128 * i + 128, :].astype(F32).astype(BF16)
        d_t[:, 128 * i : 128 * i + 128] = jnp.transpose(piece)

    def clear(n, carry):
        acc[n] = jnp.zeros(acc.shape[1:], F32)
        return carry

    lax.fori_loop(0, N_CHUNK, clear, 0)
    py_sc[...] = jnp.zeros(py_sc.shape, F32)
    corr_sc[...] = jnp.zeros(corr_sc.shape, F32)
    pp_sc[...] = jnp.zeros(pp_sc.shape, F32)
    gram = gsnd[:, 0:8]
    for d in range(1, N_GENE):
        gram_copy(d).wait_recv()
        gram = gram + grcv[d - 1, :, 0:8]
    factor = ldl(gram)
    rhs = rsnd[0]
    for d in (3, 2, 1):
        rhs_copy(d).wait_recv()
        rhs = rhs + rrcv[d - 1]
    pbuf[g] = solve(factor, rhs)

    def props_copy(d):
        return remote(pbuf.at[g], pbuf.at[g], p_s.at[d - 1], p_r.at[d - 1], gene_of(d))

    for d in (2, 1, 3):
        props_copy(d).start()

    def quarter_of(d):
        return (g + N_GENE - d) % N_GENE

    def span_of(d):
        return pl.ds(pl.multiple_of(quarter_of(d) * quarter, quarter), quarter)

    def design(d):
        props = pbuf[quarter_of(d)]
        props_ref[:, span_of(d)] = props[0:types]
        top = props.astype(BF16).astype(F32)
        des[d, 896:912, :] = jnp.concatenate([top, props - top], axis=0).astype(BF16)
        for k in range(types):
            wide = jnp.broadcast_to(top[k : k + 1, :], (16, quarter)).astype(BF16)
            for bb in range(2):
                for aa in range(2):
                    for zz in range(2):
                        source = ((2 * bb + (aa + bb) % 2) * 2 + zz) * 16
                        target = (((bb * 2 + aa) * 2 + zz) * types + k) * 16
                        des[d, target : target + 16, :] = d_t[source : source + 16, span_of(d)] * wide

    def small_term(d):
        props = pbuf[quarter_of(d)]
        top = props.astype(BF16).astype(F32)
        highs, lows = [], []
        for k in range(types):
            weight = jnp.broadcast_to(top[k : k + 1, :], (8, quarter)) * props
            high = weight.astype(BF16).astype(F32)
            highs.append(high)
            lows.append(weight - high)
        w = jnp.concatenate(highs + lows, axis=0).astype(BF16)
        corr = lax.dot_general(d_t[:, span_of(d)], w, NT, preferred_element_type=F32)
        both = des[d, 896:912, :]
        pp = lax.dot_general(both, both, NT, preferred_element_type=F32)
        corr_sc[:, 0 : 16 * types] += corr
        pp_sc[:, 0:16] += pp[0:8] + pp[8:16]

    def term(n, d):
        columns = pl.ds(pl.multiple_of(n * n_cols, n_cols), n_cols)
        value = jnp.dot(des[d], e_v[span_of(d), columns], preferred_element_type=F32)
        acc[n] += value[0:896].reshape(acc.shape[1:])
        py_sc[n] += value[896:904] + value[904:912]

    def core_copy(n):
        return remote(acc.at[n, :, :, :, :, 1 - c], rc.at[n], c_s.at[n], c_r.at[n], {"sample": core})

    def halving(n, part, step):
        axes = ORDERS[(part + n) % 3]
        ks = slice(*PARTS[part])
        kept = {axis: place[axis] for axis in axes[:step]}
        axis = axes[step]

        def block(fixed):
            return (n,) + tuple(fixed.get(name, slice(None)) for name in "baz") + (ks, c)

        landing = ((r1, r2, r3)[step])[part].at[n]
        copy = remote(
            acc.at[block({**kept, axis: 1 - place[axis]})],
            landing,
            h_s.at[n, part, step],
            h_r.at[n, part, step],
            {"sample": other[axis]},
        )
        return copy, block({**kept, axis: place[axis]}), landing

    def across(n):
        core_copy(n).wait_recv()
        acc[n, :, :, :, :, c] += rc[n]
        for part in range(3):
            halving(n, part, 0)[0].start()

    def onward(n, step):
        for part in range(3):
            copy, kept, landing = halving(n, part, step)
            copy.wait_recv()
            acc[kept] += landing[...]
            halving(n, part, step + 1)[0].start()

    def tile_copy(d):
        return remote(tsrc.at[(s + d) % N_SAMPLE], trcv.at[d - 1], t_s.at[d - 1], t_r.at[d - 1], sample_of(d))

    def spread_copy(d):
        return remote(tbuf.at[s], tbuf.at[s], u_s.at[d - 1], u_r.at[d - 1], sample_of(d))

    def start_tiles(d, carry):
        tile_copy(d).start()
        return carry

    def take_tile(d, carry):
        tile_copy(d).wait_recv()
        return carry + trcv[d - 1]

    def start_spread(d, carry):
        spread_copy(d).start()
        return carry

    def take_spread(d, carry):
        spread_copy(d).wait_recv()
        return carry

    spot = lax.broadcasted_iota(jnp.int32, (8, 128), 1)
    n_kj = 8 * types

    def send_tiles():
        pp = pp_sc[...]
        pp = pltpu.roll(pp + pltpu.roll(pp, 120, 1), n_kj, 1)
        for i in range(N_SAMPLE):
            corr = corr_sc[8 * i : 8 * i + 8, :]
            corr = corr + pltpu.roll(corr, 128 - n_kj, 1)
            at = 64 * i
            py = py_sc[at // n_cols, :, at % n_cols // 128 * 128 : at % n_cols // 128 * 128 + 128]
            if i % 2 == 0:
                py = pltpu.roll(py, 64, 1)
            tsrc[i] = jnp.where(spot < n_kj, corr, jnp.where(spot < 64, pp, py))
        lax.fori_loop(1, N_SAMPLE, start_tiles, 0)

    def spread_tiles():
        total = lax.fori_loop(1, N_SAMPLE, take_tile, tsrc[s])
        tbuf[s] = total
        lax.fori_loop(1, N_SAMPLE, start_spread, 0)
        corr_sc[0:8, :] = total
        inv, inv_t, diag = ldl(pltpu.roll(total, 128 - n_kj, 1)[:, 0:8])
        fac_sc[0, :, 0:8] = inv
        fac_sc[1, :, 0:8] = inv_t
        fac_sc[2, :, 0:1] = diag

    def solve_coef():
        lax.fori_loop(1, N_SAMPLE, take_spread, 0)
        factor = fac_sc[0, :, 0:8], fac_sc[1, :, 0:8], fac_sc[2, :, 0:1]
        tiles = [jnp.where(spot < 64, pltpu.roll(tbuf[2 * i], 64, 1), tbuf[2 * i + 1]) for i in range(n_tiles)]
        m_sc[...] = solve(factor, jnp.concatenate(tiles, axis=1))

    def finish(n):
        corr = corr_sc[0:8, :]
        coef = m_sc[:, n * n_cols : (n + 1) * n_cols]
        for part in range(3):
            copy, kept, landing = halving(n, part, 2)
            copy.wait_recv()
            value = acc[kept] + landing[...]
            for k in range(*PARTS[part]):
                out = value[k - PARTS[part][0]]
                for j in range(types):
                    out = out - corr[:, 8 * k + j : 8 * k + j + 1] * coef[j : j + 1, :]
                out = out * scale
                for i in range(per_chunk):
                    mix[n * per_chunk + i, pl.ds(k, 8, stride=types), :] = out[:, 128 * i : 128 * i + 128]
        for i in range(n * per_chunk, (n + 1) * per_chunk):
            inter_ref[:, 128 * i : 128 * i + 128] = mix[i]

    design(0)

    def step(e, carry):
        rest = (e + 12) // 16
        n = (1 - rest) * e + rest * ((e - 4) // 3)
        t = rest * (1 + (e - 4) % 3)

        @pl.when(e == 4)
        def _():
            for d in (1, 3, 2):
                props_copy(d).wait_recv()
                design(d)

        term(n, t)

        for chunk in range(N_CHUNK):
            @pl.when(e == 3 * chunk + 6)
            def _(chunk=chunk):
                core_copy(chunk).start()

        @pl.when(e == 3)
        def _():
            small_term(0)

        for chunk in range(N_CHUNK - 1):
            @pl.when(e == 3 * chunk + 8)
            def _(chunk=chunk):
                across(chunk)

        @pl.when(e == 14)
        def _():
            onward(0, 0)

        return carry

    lax.fori_loop(0, 4 * N_CHUNK, step, 0)

    def small_more(d, carry):
        small_term(d)
        return carry

    lax.fori_loop(1, N_GENE, small_more, 0)
    across(3)
    onward(1, 0)
    send_tiles()
    onward(0, 1)
    onward(2, 0)
    onward(1, 1)
    spread_tiles()
    onward(3, 0)
    onward(2, 1)
    onward(3, 1)
    solve_coef()
    for n in range(N_CHUNK):
        finish(n)

    for d in range(1, N_GENE):
        gram_copy(d).wait_send()
        rhs_copy(d).wait_send()
        props_copy(d).wait_send()
    for n in range(N_CHUNK):
        core_copy(n).wait_send()
        for part in range(3):
            for step in range(3):
                halving(n, part, step)[0].wait_send()

    def drain_tiles(d, carry):
        tile_copy(d).wait_send()
        spread_copy(d).wait_send()
        return carry

    lax.fori_loop(1, N_SAMPLE, drain_tiles, 0)


def local(expression, profile, dosage, signature):
    s_dev, g_dev = expression.shape
    v_dev = dosage.shape[1]
    types = profile.shape[1]
    quarter, n_cols = s_dev // N_GENE, g_dev // N_CHUNK
    scale = 1.0 / math.sqrt(s_dev * N_SAMPLE)
    sig_cols = -(-signature.shape[0] // 128) * 128
    sizes = [hi - lo for lo, hi in PARTS]
    vmem, dma = pltpu.VMEM, pltpu.SemaphoreType.DMA
    inter, props_t = pl.pallas_call(
        functools.partial(kernel, scale),
        out_shape=(
            vmem((v_dev * types // N_SAMPLE, g_dev), F32),
            vmem((types, s_dev), F32),
        ),
        in_specs=[
            pl.BlockSpec(memory_space=pltpu.VMEM),
            pl.BlockSpec(memory_space=pltpu.VMEM),
            pl.BlockSpec(memory_space=pl.ANY),
            pl.BlockSpec(memory_space=pl.ANY),
        ],
        out_specs=(pl.BlockSpec(memory_space=pltpu.VMEM), pl.BlockSpec(memory_space=pltpu.VMEM)),
        scratch_shapes=[
            vmem((s_dev, g_dev), BF16),
            vmem((s_dev, v_dev), jnp.int32),
            vmem((v_dev, s_dev), BF16),
            vmem((N_GENE, v_dev * types + 16, quarter), BF16),
            vmem((1, sig_cols), jnp.int32),
            vmem((8, g_dev), F32),
            vmem((N_CHUNK, 2, 2, 2, types, 2, 8, n_cols), F32),
            vmem((N_CHUNK, 2, 2, 2, types, 8, n_cols), F32),
            [vmem((N_CHUNK, 2, 2, k, 8, n_cols), F32) for k in sizes],
            [vmem((N_CHUNK, 2, k, 8, n_cols), F32) for k in sizes],
            [vmem((N_CHUNK, k, 8, n_cols), F32) for k in sizes],
            vmem((N_GENE, 8, quarter), F32),
            vmem((N_GENE, 8, quarter), F32),
            vmem((N_GENE - 1, 8, quarter), F32),
            vmem((8, 128), F32),
            vmem((N_GENE - 1, 8, 128), F32),
            vmem((v_dev, 128), F32),
            vmem((8, 128), F32),
            vmem((N_CHUNK, 8, n_cols), F32),
            vmem((3, 8, 128), F32),
            vmem((N_SAMPLE, 8, 128), F32),
            vmem((N_SAMPLE - 1, 8, 128), F32),
            vmem((N_SAMPLE, 8, 128), F32),
            vmem((g_dev // 128, 8 * types, 128), F32),
            dma((N_GENE, 2)),
            dma,
            dma((N_GENE - 1,)),
            dma((N_GENE - 1,)),
            dma((N_GENE - 1,)),
            dma((N_GENE - 1,)),
            dma((N_GENE - 1,)),
            dma((N_GENE - 1,)),
            dma((N_CHUNK,)),
            dma((N_CHUNK,)),
            dma((N_CHUNK, 3, 3)),
            dma((N_CHUNK, 3, 3)),
            dma((N_SAMPLE - 1,)),
            dma((N_SAMPLE - 1,)),
            dma((N_SAMPLE - 1,)),
            dma((N_SAMPLE - 1,)),
        ],
        compiler_params=pltpu.CompilerParams(
            collective_id=0, has_side_effects=True, vmem_limit_bytes=VMEM_BYTES
        ),
        name="eqtl",
    )(signature.reshape(1, -1), profile.T, expression, dosage)
    return inter, props_t.T


def solution(mesh):
    placed = (P("sample", "gene"), P("gene", None), P("sample", "variant"), P())
    return jax.shard_map(
        local,
        mesh=mesh,
        in_specs=placed,
        out_specs=(P(("variant", "sample"), "gene"), P("sample", None)),
        check_vma=False,
    )
```

time: 52.9 us -> 45.6 us (0.86); the launches traced: 51.9 us -> 45.5 us
  Pallas kernels: 48 us -> 43.5 us
  local copies, waits for them, and re-layouts: 3.21 us -> 1.35 us
    pallas_call x1, Pallas kernels: 48 us -> 43.5 us  [local(): pl.pallas_call(functools.partial(kernel, scale), out_shape=(vmem((v_dev *...]
    unnamed x2, local copies, waits for them, and re-layouts: 3.21 us -> 1.35 us
where the time goes in v2:
time: 45.6 us; the launch traced here: 45.5 us
  Pallas kernels  43.5 us (95%)
  local copies, waits for them, and re-layouts  1.35 us (3%)
  between operations  0.64 us (1%)
    pallas_call x1, Pallas kernels, local(): pl.pallas_call(functools.partial(kernel, scale), out_shape=(vmem((v_dev *...  43.5 us
    unnamed x2, local copies, waits for them, and re-layouts  1.35 us

profile of v2, /device:TPU:64, one launch (start us, length us, event | category | flops | bytes accessed | tf_op | source)
XLA Modules:
  0.0 45.5 jit_solution(3055212910317566333)
XLA Ops:
  0.6 43.5 %eqtl.1 = (f32[56,1024]{1,0:T(8,128)S(1)}, f32[7,4096]{1,0:T(8,128)S(1)}) custom-call(s32[1,500]{1,0:T(1,128)} %bitcast.5, f32[7,1024]{1,0:T(8,128)} %bitcast.4, bf16[4096,1024]{1,0:T(8,128)(2,1)} %expr_hbm.1, s32[4096,128]{1,0:T(8,128)} %dos_hbm.1), custom_call_target="tpu_custom_call" | custom-call | tf_op jit(solution)/shard_map/eqtl/pallas_call | solution.py:420
  44.1 0.7 %copy.8 = f32[56,1024]{1,0:T(8,128)} copy(f32[56,1024]{1,0:T(8,128)S(1)} %get-tuple-element.6) | data formatting | bytes 458752
  44.8 0.7 %copy.9 = f32[4096,7]{0,1:T(8,128)} copy(f32[4096,7]{0,1:T(8,128)S(1)} %bitcast.3) | data formatting | bytes 229376

commit v3 on v2

--- a/solution.py
+++ b/solution.py
@@ -51,11 +51,11 @@
 
 def kernel(
     scale,
-    sig_ref, prof_ref, expr_hbm, dos_hbm,
+    sig_hbm, prof_hbm, expr_hbm, dos_hbm,
     inter_ref, props_ref,
-    e_v, d_v, d_t, des, sig_sc, m_sc, acc, rc, r1, r2, r3,
+    e_v, d_v, d_t, des, sig_ref, prof_ref, sig_sc, m_sc, acc, rc, r1, r2, r3,
     pbuf, rsnd, rrcv, gsnd, grcv, corr_sc, pp_sc, py_sc, fac_sc, tsrc, trcv, tbuf, mix,
-    e_sem, d_sem, g_s, g_r, x_s, x_r, p_s, p_r, c_s, c_r, h_s, h_r, t_s, t_r, u_s, u_r,
+    e_sem, d_sem, i_sem, g_s, g_r, x_s, x_r, p_s, p_r, c_s, c_r, h_s, h_r, t_s, t_r, u_s, u_r,
 ):
     s_dev, g_dev = e_v.shape
     quarter = s_dev // N_GENE
@@ -83,22 +83,32 @@
     def sample_of(d):
         return {"sample": (s + d) % N_SAMPLE}
 
-    def rows_of(d, h):
-        return pl.ds(pl.multiple_of(((g + d) % N_GENE) * quarter + h * half, half), half)
+    def quarter_of(d):
+        return (g + N_GENE - d) % N_GENE
 
     def load(d, h):
-        return pltpu.make_async_copy(expr_hbm.at[rows_of(d, h), :], e_v.at[rows_of(d, h), :], e_sem.at[d, h])
+        source = pl.ds(pl.multiple_of(quarter_of(d) * quarter + h * half, half), half)
+        target = pl.ds(pl.multiple_of(d * quarter + h * half, half), half)
+        return pltpu.make_async_copy(expr_hbm.at[source, :], e_v.at[target, :], e_sem.at[d, h])
+
+    def load_dosage(d):
+        source = pl.ds(pl.multiple_of(quarter_of(d) * quarter, quarter), quarter)
+        return pltpu.make_async_copy(dos_hbm.at[source, :], d_v.at[pl.ds(d * quarter, quarter), :], d_sem.at[d])
 
     def remote(src, dst, send, recv, device):
         return pltpu.make_async_remote_copy(
             src_ref=src, dst_ref=dst, send_sem=send, recv_sem=recv, device_id=device, device_id_type=MESH
         )
 
-    for d in (3, 2, 1, 0):
+    sig_copy = pltpu.make_async_copy(sig_hbm, sig_ref, i_sem.at[0])
+    prof_copy = pltpu.make_async_copy(prof_hbm, prof_ref, i_sem.at[1])
+    sig_copy.start()
+    prof_copy.start()
+    for d in (1, 2, 3, 0):
         for h in range(2):
             load(d, h).start()
-    dos_copy = pltpu.make_async_copy(dos_hbm, d_v, d_sem)
-    dos_copy.start()
+    for d in range(N_GENE):
+        load_dosage(d).start()
 
     barrier = pltpu.get_barrier_semaphore()
     for d in range(1, N_GENE):
@@ -108,6 +118,7 @@
 
     n_sig = sig_ref.shape[1]
     sig_sc[...] = jnp.full(sig_sc.shape, -1, jnp.int32)
+    sig_copy.wait()
     sig_sc[0:1, 0:n_sig] = sig_ref[...]
     cols = []
     for t in range(sig_sc.shape[1] // 128):
@@ -115,6 +126,7 @@
         cols.append(jnp.transpose(jnp.broadcast_to(line, (128, 128))))
     lane = lax.broadcasted_iota(jnp.int32, (128, 128), 1) + g * g_dev
     m_sc[...] = jnp.zeros(m_sc.shape, F32)
+    prof_copy.wait()
     for t in range(n_tiles):
         ids = (lane + 128 * t).astype(F32)
         hit = jnp.zeros((128, 128), F32)
@@ -138,8 +150,10 @@
 
     def rhs_half(i, carry):
         d, h = N_GENE - 1 - i // 2, i % 2
-        load(d, h).wait()
-        part = lax.dot_general(m3, e_v[rows_of(d, h), :], NT, preferred_element_type=F32)
+        at = (N_GENE - d) % N_GENE
+        load(at, h).wait()
+        rows = pl.ds(pl.multiple_of(at * quarter + h * half, half), half)
+        part = lax.dot_general(m3, e_v[rows, :], NT, preferred_element_type=F32)
         rsnd[d, :, pl.ds(pl.multiple_of(h * half, half), half)] = part[0:8] + part[8:16] + part[16:24]
 
         @pl.when(i == 1)
@@ -156,17 +170,11 @@
 
     lax.fori_loop(0, 2 * N_GENE, rhs_half, 0)
 
-    dos_copy.wait()
+    for d in range(N_GENE):
+        load_dosage(d).wait()
     for i in range(s_dev // 128):
         piece = d_v[128 * i : 128 * i + 128, :].astype(F32).astype(BF16)
         d_t[:, 128 * i : 128 * i + 128] = jnp.transpose(piece)
-
-    def clear(n, carry):
-        acc[n] = jnp.zeros(acc.shape[1:], F32)
-        return carry
-
-    lax.fori_loop(0, N_CHUNK, clear, 0)
-    py_sc[...] = jnp.zeros(py_sc.shape, F32)
     corr_sc[...] = jnp.zeros(corr_sc.shape, F32)
     pp_sc[...] = jnp.zeros(pp_sc.shape, F32)
     gram = gsnd[:, 0:8]
@@ -186,17 +194,14 @@
     for d in (2, 1, 3):
         props_copy(d).start()
 
-    def quarter_of(d):
-        return (g + N_GENE - d) % N_GENE
-
     def span_of(d):
-        return pl.ds(pl.multiple_of(quarter_of(d) * quarter, quarter), quarter)
+        return slice(d * quarter, (d + 1) * quarter)
 
     def design(d):
         props = pbuf[quarter_of(d)]
-        props_ref[:, span_of(d)] = props[0:types]
+        props_ref[:, pl.ds(pl.multiple_of(quarter_of(d) * quarter, quarter), quarter)] = props[0:types]
         top = props.astype(BF16).astype(F32)
-        des[d, 896:912, :] = jnp.concatenate([top, props - top], axis=0).astype(BF16)
+        des[896:912, span_of(d)] = jnp.concatenate([top, props - top], axis=0).astype(BF16)
         for k in range(types):
             wide = jnp.broadcast_to(top[k : k + 1, :], (16, quarter)).astype(BF16)
             for bb in range(2):
@@ -204,9 +209,10 @@
                     for zz in range(2):
                         source = ((2 * bb + (aa + bb) % 2) * 2 + zz) * 16
                         target = (((bb * 2 + aa) * 2 + zz) * types + k) * 16
-                        des[d, target : target + 16, :] = d_t[source : source + 16, span_of(d)] * wide
+                        des[target : target + 16, span_of(d)] = d_t[source : source + 16, span_of(d)] * wide
 
     def small_term(d):
+        span = pl.ds(pl.multiple_of(d * quarter, quarter), quarter)
         props = pbuf[quarter_of(d)]
         top = props.astype(BF16).astype(F32)
         highs, lows = [], []
@@ -216,17 +222,19 @@
             highs.append(high)
             lows.append(weight - high)
         w = jnp.concatenate(highs + lows, axis=0).astype(BF16)
-        corr = lax.dot_general(d_t[:, span_of(d)], w, NT, preferred_element_type=F32)
-        both = des[d, 896:912, :]
+        corr = lax.dot_general(d_t[:, span], w, NT, preferred_element_type=F32)
+        both = des[896:912, span]
         pp = lax.dot_general(both, both, NT, preferred_element_type=F32)
         corr_sc[:, 0 : 16 * types] += corr
         pp_sc[:, 0:16] += pp[0:8] + pp[8:16]
 
-    def term(n, d):
+    def term(n, first):
         columns = pl.ds(pl.multiple_of(n * n_cols, n_cols), n_cols)
-        value = jnp.dot(des[d], e_v[span_of(d), columns], preferred_element_type=F32)
-        acc[n] += value[0:896].reshape(acc.shape[1:])
-        py_sc[n] += value[896:904] + value[904:912]
+        span = slice(0, quarter) if first else slice(quarter, s_dev)
+        value = jnp.dot(des[:, span], e_v[span, columns], preferred_element_type=F32)
+        body, tail = value[0:896].reshape(acc.shape[1:]), value[896:904] + value[904:912]
+        acc[n] = body if first else acc[n] + body
+        py_sc[n] = tail if first else py_sc[n] + tail
 
     def core_copy(n):
         return remote(acc.at[n, :, :, :, :, 1 - c], rc.at[n], c_s.at[n], c_r.at[n], {"sample": core})
@@ -336,54 +344,42 @@
 
     design(0)
 
-    def step(e, carry):
-        rest = (e + 12) // 16
-        n = (1 - rest) * e + rest * ((e - 4) // 3)
-        t = rest * (1 + (e - 4) % 3)
-
-        @pl.when(e == 4)
-        def _():
-            for d in (1, 3, 2):
-                props_copy(d).wait_recv()
-                design(d)
-
-        term(n, t)
-
-        for chunk in range(N_CHUNK):
-            @pl.when(e == 3 * chunk + 6)
+    def own(n, carry):
+        term(n, True)
+        return carry
+
+    lax.fori_loop(0, N_CHUNK, own, 0)
+    small_term(0)
+    for d in (1, 3, 2):
+        props_copy(d).wait_recv()
+        design(d)
+
+    def others(n, carry):
+        term(n, False)
+        core_copy(n).start()
+        for chunk in range(1, N_CHUNK):
+            @pl.when(n == chunk)
             def _(chunk=chunk):
-                core_copy(chunk).start()
-
-        @pl.when(e == 3)
-        def _():
-            small_term(0)
-
-        for chunk in range(N_CHUNK - 1):
-            @pl.when(e == 3 * chunk + 8)
-            def _(chunk=chunk):
-                across(chunk)
-
-        @pl.when(e == 14)
-        def _():
-            onward(0, 0)
-
-        return carry
-
-    lax.fori_loop(0, 4 * N_CHUNK, step, 0)
+                across(chunk - 1)
+
+        return carry
+
+    lax.fori_loop(0, N_CHUNK, others, 0)
 
     def small_more(d, carry):
         small_term(d)
         return carry
 
     lax.fori_loop(1, N_GENE, small_more, 0)
+    onward(0, 0)
     across(3)
+    send_tiles()
     onward(1, 0)
-    send_tiles()
     onward(0, 1)
     onward(2, 0)
+    onward(3, 0)
+    spread_tiles()
     onward(1, 1)
-    spread_tiles()
-    onward(3, 0)
     onward(2, 1)
     onward(3, 1)
     solve_coef()
@@ -424,8 +420,8 @@
             vmem((types, s_dev), F32),
         ),
         in_specs=[
-            pl.BlockSpec(memory_space=pltpu.VMEM),
-            pl.BlockSpec(memory_space=pltpu.VMEM),
+            pl.BlockSpec(memory_space=pl.ANY),
+            pl.BlockSpec(memory_space=pl.ANY),
             pl.BlockSpec(memory_space=pl.ANY),
             pl.BlockSpec(memory_space=pl.ANY),
         ],
@@ -434,7 +430,9 @@
             vmem((s_dev, g_dev), BF16),
             vmem((s_dev, v_dev), jnp.int32),
             vmem((v_dev, s_dev), BF16),
-            vmem((N_GENE, v_dev * types + 16, quarter), BF16),
+            vmem((v_dev * types + 16, s_dev), BF16),
+            vmem((1, signature.shape[0]), jnp.int32),
+            vmem((types, g_dev), F32),
             vmem((1, sig_cols), jnp.int32),
             vmem((8, g_dev), F32),
             vmem((N_CHUNK, 2, 2, 2, types, 2, 8, n_cols), F32),
@@ -456,7 +454,8 @@
             vmem((N_SAMPLE, 8, 128), F32),
             vmem((g_dev // 128, 8 * types, 128), F32),
             dma((N_GENE, 2)),
-            dma,
+            dma((N_GENE,)),
+            dma((2,)),
             dma((N_GENE - 1,)),
             dma((N_GENE - 1,)),
             dma((N_GENE - 1,)),

time: 45.6 us -> 42.5 us (0.932)
  the two profiles are of different devices: /device:TPU:64 before, /device:TPU:1 now
where the time goes in v3:
time: 42.5 us; the launch traced here: 42.4 us
  Pallas kernels  40.4 us (95%)
  local copies, waits for them, and re-layouts  1.35 us (3%)
  between operations  0.64 us (2%)
    pallas_call x1, Pallas kernels, local(): pl.pallas_call(functools.partial(kernel, scale), out_shape=(vmem((v_dev *...  40.4 us
    unnamed x2, local copies, waits for them, and re-layouts  1.35 us

profile of v3, /device:TPU:1, one launch (start us, length us, event | category | flops | bytes accessed | tf_op | source)
XLA Modules:
  0.0 42.4 jit_solution(11879632167137586515)
XLA Ops:
  0.6 40.4 %eqtl.1 = (f32[56,1024]{1,0:T(8,128)S(1)}, f32[7,4096]{1,0:T(8,128)S(1)}) custom-call(s32[1,500]{1,0:T(1,128)} %bitcast.5, f32[7,1024]{1,0:T(8,128)} %bitcast.4, bf16[4096,1024]{1,0:T(8,128)(2,1)} %expr_hbm.1, s32[4096,128]{1,0:T(8,128)} %dos_hbm.1), custom_call_target="tpu_custom_call" | custom-call | tf_op jit(solution)/shard_map/eqtl/pallas_call | solution.py:416
  41.1 0.7 %copy.8 = f32[56,1024]{1,0:T(8,128)} copy(f32[56,1024]{1,0:T(8,128)S(1)} %get-tuple-element.6) | data formatting | bytes 458752
  41.7 0.7 %copy.9 = f32[4096,7]{0,1:T(8,128)} copy(f32[4096,7]{0,1:T(8,128)S(1)} %bitcast.3) | data formatting | bytes 229376

commit v4 on v3

--- a/solution.py
+++ b/solution.py
@@ -55,7 +55,7 @@
     inter_ref, props_ref,
     e_v, d_v, d_t, des, sig_ref, prof_ref, sig_sc, m_sc, acc, rc, r1, r2, r3,
     pbuf, rsnd, rrcv, gsnd, grcv, corr_sc, pp_sc, py_sc, fac_sc, tsrc, trcv, tbuf, mix,
-    e_sem, d_sem, i_sem, g_s, g_r, x_s, x_r, p_s, p_r, c_s, c_r, h_s, h_r, t_s, t_r, u_s, u_r,
+    e_sem, d_sem, i_sem, sent, g_r, x_r, p_r, c_r, h_r, t_r, u_r,
 ):
     s_dev, g_dev = e_v.shape
     quarter = s_dev // N_GENE
@@ -95,20 +95,17 @@
         source = pl.ds(pl.multiple_of(quarter_of(d) * quarter, quarter), quarter)
         return pltpu.make_async_copy(dos_hbm.at[source, :], d_v.at[pl.ds(d * quarter, quarter), :], d_sem.at[d])
 
-    def remote(src, dst, send, recv, device):
+    def remote(src, dst, recv, device):
         return pltpu.make_async_remote_copy(
-            src_ref=src, dst_ref=dst, send_sem=send, recv_sem=recv, device_id=device, device_id_type=MESH
+            src_ref=src, dst_ref=dst, send_sem=sent, recv_sem=recv, device_id=device, device_id_type=MESH
         )
 
     sig_copy = pltpu.make_async_copy(sig_hbm, sig_ref, i_sem.at[0])
     prof_copy = pltpu.make_async_copy(prof_hbm, prof_ref, i_sem.at[1])
     sig_copy.start()
     prof_copy.start()
-    for d in (1, 2, 3, 0):
-        for h in range(2):
-            load(d, h).start()
-    for d in range(N_GENE):
-        load_dosage(d).start()
+    for h in range(2):
+        load(1, h).start()
 
     barrier = pltpu.get_barrier_semaphore()
     for d in range(1, N_GENE):
@@ -119,6 +116,12 @@
     n_sig = sig_ref.shape[1]
     sig_sc[...] = jnp.full(sig_sc.shape, -1, jnp.int32)
     sig_copy.wait()
+    prof_copy.wait()
+    for d in (2, 3, 0):
+        for h in range(2):
+            load(d, h).start()
+    for d in range(N_GENE):
+        load_dosage(d).start()
     sig_sc[0:1, 0:n_sig] = sig_ref[...]
     cols = []
     for t in range(sig_sc.shape[1] // 128):
@@ -126,7 +129,6 @@
         cols.append(jnp.transpose(jnp.broadcast_to(line, (128, 128))))
     lane = lax.broadcasted_iota(jnp.int32, (128, 128), 1) + g * g_dev
     m_sc[...] = jnp.zeros(m_sc.shape, F32)
-    prof_copy.wait()
     for t in range(n_tiles):
         ids = (lane + 128 * t).astype(F32)
         hit = jnp.zeros((128, 128), F32)
@@ -143,10 +145,10 @@
     m3 = jnp.concatenate([top, mid, rest - mid], axis=0).astype(BF16)
 
     def gram_copy(d):
-        return remote(gsnd, grcv.at[d - 1], g_s.at[d - 1], g_r.at[d - 1], gene_of(d))
+        return remote(gsnd, grcv.at[d - 1], g_r.at[d - 1], gene_of(d))
 
     def rhs_copy(d):
-        return remote(rsnd.at[d], rrcv.at[d - 1], x_s.at[d - 1], x_r.at[d - 1], gene_of(d))
+        return remote(rsnd.at[d], rrcv.at[d - 1], x_r.at[d - 1], gene_of(d))
 
     def rhs_half(i, carry):
         d, h = N_GENE - 1 - i // 2, i % 2
@@ -189,7 +191,7 @@
     pbuf[g] = solve(factor, rhs)
 
     def props_copy(d):
-        return remote(pbuf.at[g], pbuf.at[g], p_s.at[d - 1], p_r.at[d - 1], gene_of(d))
+        return remote(pbuf.at[g], pbuf.at[g], p_r.at[d - 1], gene_of(d))
 
     for d in (2, 1, 3):
         props_copy(d).start()
@@ -237,7 +239,7 @@
         py_sc[n] = tail if first else py_sc[n] + tail
 
     def core_copy(n):
-        return remote(acc.at[n, :, :, :, :, 1 - c], rc.at[n], c_s.at[n], c_r.at[n], {"sample": core})
+        return remote(acc.at[n, :, :, :, :, 1 - c], rc.at[n], c_r.at[n], {"sample": core})
 
     def halving(n, part, step):
         axes = ORDERS[(part + n) % 3]
@@ -252,7 +254,6 @@
         copy = remote(
             acc.at[block({**kept, axis: 1 - place[axis]})],
             landing,
-            h_s.at[n, part, step],
             h_r.at[n, part, step],
             {"sample": other[axis]},
         )
@@ -272,25 +273,20 @@
             halving(n, part, step + 1)[0].start()
 
     def tile_copy(d):
-        return remote(tsrc.at[(s + d) % N_SAMPLE], trcv.at[d - 1], t_s.at[d - 1], t_r.at[d - 1], sample_of(d))
+        return remote(tsrc.at[(s + d) % N_SAMPLE], trcv.at[d], t_r, sample_of(d))
 
     def spread_copy(d):
-        return remote(tbuf.at[s], tbuf.at[s], u_s.at[d - 1], u_r.at[d - 1], sample_of(d))
+        return remote(tbuf.at[0], tbuf.at[d], u_r, sample_of(d))
 
     def start_tiles(d, carry):
         tile_copy(d).start()
         return carry
 
-    def take_tile(d, carry):
-        tile_copy(d).wait_recv()
-        return carry + trcv[d - 1]
+    def wait_tiles(buffer, recv):
+        remote(tsrc.at[1:N_SAMPLE], buffer.at[1:N_SAMPLE], recv, sample_of(1)).wait_recv()
 
     def start_spread(d, carry):
         spread_copy(d).start()
-        return carry
-
-    def take_spread(d, carry):
-        spread_copy(d).wait_recv()
         return carry
 
     spot = lax.broadcasted_iota(jnp.int32, (8, 128), 1)
@@ -310,8 +306,11 @@
         lax.fori_loop(1, N_SAMPLE, start_tiles, 0)
 
     def spread_tiles():
-        total = lax.fori_loop(1, N_SAMPLE, take_tile, tsrc[s])
-        tbuf[s] = total
+        wait_tiles(trcv, t_r)
+        total = tsrc[s]
+        for d in range(1, N_SAMPLE):
+            total = total + trcv[d]
+        tbuf[0] = total
         lax.fori_loop(1, N_SAMPLE, start_spread, 0)
         corr_sc[0:8, :] = total
         inv, inv_t, diag = ldl(pltpu.roll(total, 128 - n_kj, 1)[:, 0:8])
@@ -320,9 +319,10 @@
         fac_sc[2, :, 0:1] = diag
 
     def solve_coef():
-        lax.fori_loop(1, N_SAMPLE, take_spread, 0)
+        wait_tiles(tbuf, u_r)
         factor = fac_sc[0, :, 0:8], fac_sc[1, :, 0:8], fac_sc[2, :, 0:1]
-        tiles = [jnp.where(spot < 64, pltpu.roll(tbuf[2 * i], 64, 1), tbuf[2 * i + 1]) for i in range(n_tiles)]
+        own = [tbuf[(s + N_SAMPLE - i) % N_SAMPLE] for i in range(N_SAMPLE)]
+        tiles = [jnp.where(spot < 64, pltpu.roll(own[2 * i], 64, 1), own[2 * i + 1]) for i in range(n_tiles)]
         m_sc[...] = solve(factor, jnp.concatenate(tiles, axis=1))
 
     def finish(n):
@@ -349,14 +349,19 @@
         return carry
 
     lax.fori_loop(0, N_CHUNK, own, 0)
-    small_term(0)
     for d in (1, 3, 2):
         props_copy(d).wait_recv()
         design(d)
 
     def others(n, carry):
         term(n, False)
+        small_term(n)
         core_copy(n).start()
+
+        @pl.when(n == N_CHUNK - 1)
+        def _():
+            send_tiles()
+
         for chunk in range(1, N_CHUNK):
             @pl.when(n == chunk)
             def _(chunk=chunk):
@@ -366,25 +371,21 @@
 
     lax.fori_loop(0, N_CHUNK, others, 0)
 
-    def small_more(d, carry):
-        small_term(d)
-        return carry
-
-    lax.fori_loop(1, N_GENE, small_more, 0)
     onward(0, 0)
     across(3)
-    send_tiles()
     onward(1, 0)
+    spread_tiles()
     onward(0, 1)
     onward(2, 0)
     onward(3, 0)
-    spread_tiles()
     onward(1, 1)
     onward(2, 1)
+    solve_coef()
+    finish(0)
     onward(3, 1)
-    solve_coef()
-    for n in range(N_CHUNK):
-        finish(n)
+    finish(1)
+    finish(2)
+    finish(3)
 
     for d in range(1, N_GENE):
         gram_copy(d).wait_send()
@@ -450,26 +451,20 @@
             vmem((N_CHUNK, 8, n_cols), F32),
             vmem((3, 8, 128), F32),
             vmem((N_SAMPLE, 8, 128), F32),
-            vmem((N_SAMPLE - 1, 8, 128), F32),
+            vmem((N_SAMPLE, 8, 128), F32),
             vmem((N_SAMPLE, 8, 128), F32),
             vmem((g_dev // 128, 8 * types, 128), F32),
             dma((N_GENE, 2)),
             dma((N_GENE,)),
             dma((2,)),
-            dma((N_GENE - 1,)),
-            dma((N_GENE - 1,)),
-            dma((N_GENE - 1,)),
+            dma,
             dma((N_GENE - 1,)),
             dma((N_GENE - 1,)),
             dma((N_GENE - 1,)),
             dma((N_CHUNK,)),
-            dma((N_CHUNK,)),
             dma((N_CHUNK, 3, 3)),
-            dma((N_CHUNK, 3, 3)),
-            dma((N_SAMPLE - 1,)),
-            dma((N_SAMPLE - 1,)),
-            dma((N_SAMPLE - 1,)),
-            dma((N_SAMPLE - 1,)),
+            dma,
+            dma,
         ],
         compiler_params=pltpu.CompilerParams(
             collective_id=0, has_side_effects=True, vmem_limit_bytes=VMEM_BYTES

time: 42.5 us -> 39.6 us (0.932)
  the two profiles are of different devices: /device:TPU:1 before, /device:TPU:64 now
where the time goes in v4:
time: 39.6 us; the launch traced here: 39.5 us
  Pallas kernels  37.5 us (95%)
  local copies, waits for them, and re-layouts  1.35 us (3%)
  between operations  0.64 us (2%)
    pallas_call x1, Pallas kernels, local(): pl.pallas_call(functools.partial(kernel, scale), out_shape=(vmem((v_dev *...  37.5 us
    unnamed x2, local copies, waits for them, and re-layouts  1.35 us

profile of v4, /device:TPU:64, one launch (start us, length us, event | category | flops | bytes accessed | tf_op | source)
XLA Modules:
  0.0 39.5 jit_solution(14712187287977815626)
XLA Ops:
  0.6 37.5 %eqtl.1 = (f32[56,1024]{1,0:T(8,128)S(1)}, f32[7,4096]{1,0:T(8,128)S(1)}) custom-call(s32[1,500]{1,0:T(1,128)} %bitcast.5, f32[7,1024]{1,0:T(8,128)} %bitcast.4, bf16[4096,1024]{1,0:T(8,128)(2,1)} %expr_hbm.1, s32[4096,128]{1,0:T(8,128)} %dos_hbm.1), custom_call_target="tpu_custom_call" | custom-call | tf_op jit(solution)/shard_map/eqtl/pallas_call | solution.py:417
  38.2 0.7 %copy.8 = f32[56,1024]{1,0:T(8,128)} copy(f32[56,1024]{1,0:T(8,128)S(1)} %get-tuple-element.6) | data formatting | bytes 458752
  38.8 0.7 %copy.9 = f32[4096,7]{0,1:T(8,128)} copy(f32[4096,7]{0,1:T(8,128)S(1)} %bitcast.3) | data formatting | bytes 229376

commit v5 on v4

--- a/solution.py
+++ b/solution.py
@@ -17,7 +17,29 @@
 N_CHUNK = 4
 VMEM_BYTES = 62_000_000
 PARTS = ((0, 2), (2, 4), (4, 7))
-ORDERS = ("abz", "zab", "bza")
+ORDERS = (
+    ("abz", "zab", "baz"),
+    ("azb", "zab", "zab"),
+    ("bza", "abz", "abz"),
+    ("zba", "zab", "bza"),
+)
+DURING = {
+    (1, 0): ((0, 0, -1),),
+    (1, 1): ((0, 1, -1),),
+    (1, 2): ((0, 2, -1), (1, 0, -1)),
+    (2, 0): ((1, 1, -1),),
+    (2, 2): ((1, 2, -1), (0, 0, 0), (2, 0, -1), (0, 1, 0)),
+    (3, 0): ((2, 1, -1),),
+    (3, 1): ((1, 0, 0),),
+}
+AFTER = (
+    (2, 2, -1), (1, 1, 0), (0, 2, 0), (3, 0, -1), (3, 1, -1), (0, 0, 1), (0, 1, 1), (3, 2, -1), (1, 2, 0), (2, 0, 0),
+    (2, 1, 0), (1, 0, 1), (3, 0, 0), (2, 2, 0), (3, 2, 0), (1, 1, 1), (3, 1, 0), "spread", (2, 1, 1), (0, 2, 1),
+    (2, 0, 1), (3, 0, 1), (1, 2, 1), (3, 2, 1), (2, 2, 1), (3, 1, 1),
+)
+LAST = (
+    (0, 0), (0, 1), (1, 0), (0, 2), (2, 1), (1, 1), (2, 0), (1, 2), (3, 0), (3, 2), (2, 2), (3, 1),
+)
 
 
 def ldl(gram):
@@ -147,8 +169,8 @@
     def gram_copy(d):
         return remote(gsnd, grcv.at[d - 1], g_r.at[d - 1], gene_of(d))
 
-    def rhs_copy(d):
-        return remote(rsnd.at[d], rrcv.at[d - 1], x_r.at[d - 1], gene_of(d))
+    def rhs_copy(d, h):
+        return remote(rsnd.at[d, h], rrcv.at[d - 1, h], x_r.at[d - 1, h], gene_of(d))
 
     def rhs_half(i, carry):
         d, h = N_GENE - 1 - i // 2, i % 2
@@ -156,17 +178,17 @@
         load(at, h).wait()
         rows = pl.ds(pl.multiple_of(at * quarter + h * half, half), half)
         part = lax.dot_general(m3, e_v[rows, :], NT, preferred_element_type=F32)
-        rsnd[d, :, pl.ds(pl.multiple_of(h * half, half), half)] = part[0:8] + part[8:16] + part[16:24]
-
-        @pl.when(i == 1)
+        rsnd[d, h] = part[0:8] + part[8:16] + part[16:24]
+
+        @pl.when(i == 0)
         def _():
             pl.semaphore_wait(barrier, N_GENE - 1 + N_SAMPLE - 1)
             for peer in range(1, N_GENE):
                 gram_copy(peer).start()
 
-        @pl.when((h == 1) & (d > 0))
+        @pl.when(d > 0)
         def _():
-            rhs_copy(d).start()
+            rhs_copy(d, h).start()
 
         return carry
 
@@ -184,11 +206,11 @@
         gram_copy(d).wait_recv()
         gram = gram + grcv[d - 1, :, 0:8]
     factor = ldl(gram)
-    rhs = rsnd[0]
     for d in (3, 2, 1):
-        rhs_copy(d).wait_recv()
-        rhs = rhs + rrcv[d - 1]
-    pbuf[g] = solve(factor, rhs)
+        for h in range(2):
+            rhs_copy(d, h).wait_recv()
+    for h in range(2):
+        pbuf[g, :, h * half : (h + 1) * half] = solve(factor, rsnd[0, h] + rrcv[2, h] + rrcv[1, h] + rrcv[0, h])
 
     def props_copy(d):
         return remote(pbuf.at[g], pbuf.at[g], p_r.at[d - 1], gene_of(d))
@@ -205,12 +227,13 @@
         top = props.astype(BF16).astype(F32)
         des[896:912, span_of(d)] = jnp.concatenate([top, props - top], axis=0).astype(BF16)
         for k in range(types):
+            lo, hi = [part for part in PARTS if part[0] <= k < part[1]][0]
             wide = jnp.broadcast_to(top[k : k + 1, :], (16, quarter)).astype(BF16)
             for bb in range(2):
                 for aa in range(2):
                     for zz in range(2):
                         source = ((2 * bb + (aa + bb) % 2) * 2 + zz) * 16
-                        target = (((bb * 2 + aa) * 2 + zz) * types + k) * 16
+                        target = lo * 128 + (((bb * 2 + aa) * 2 + zz) * (hi - lo) + k - lo) * 16
                         des[target : target + 16, span_of(d)] = d_t[source : source + 16, span_of(d)] * wide
 
     def small_term(d):
@@ -230,47 +253,51 @@
         corr_sc[:, 0 : 16 * types] += corr
         pp_sc[:, 0:16] += pp[0:8] + pp[8:16]
 
-    def term(n, first):
+    def term(n, part, first):
         columns = pl.ds(pl.multiple_of(n * n_cols, n_cols), n_cols)
         span = slice(0, quarter) if first else slice(quarter, s_dev)
-        value = jnp.dot(des[:, span], e_v[span, columns], preferred_element_type=F32)
-        body, tail = value[0:896].reshape(acc.shape[1:]), value[896:904] + value[904:912]
-        acc[n] = body if first else acc[n] + body
-        py_sc[n] = tail if first else py_sc[n] + tail
-
-    def core_copy(n):
-        return remote(acc.at[n, :, :, :, :, 1 - c], rc.at[n], c_r.at[n], {"sample": core})
+        lo, hi = PARTS[part]
+        size = 128 * (hi - lo)
+        last = part == len(PARTS) - 1
+        rows = slice(128 * lo, 128 * hi + (16 if last else 0))
+        value = jnp.dot(des[rows, span], e_v[span, columns], preferred_element_type=F32)
+        body = value[0:size].reshape(acc[part].shape[1:])
+        acc[part][n] = body if first else acc[part][n] + body
+        if last:
+            tail = value[size : size + 8] + value[size + 8 : size + 16]
+            py_sc[n] = tail if first else py_sc[n] + tail
+
+    def core_copy(n, part):
+        return remote(
+            acc[part].at[n, :, :, :, :, 1 - c], rc[part].at[n], c_r.at[n, part], {"sample": core}
+        )
 
     def halving(n, part, step):
-        axes = ORDERS[(part + n) % 3]
-        ks = slice(*PARTS[part])
+        axes = ORDERS[n][part]
         kept = {axis: place[axis] for axis in axes[:step]}
         axis = axes[step]
 
         def block(fixed):
-            return (n,) + tuple(fixed.get(name, slice(None)) for name in "baz") + (ks, c)
+            return (n,) + tuple(fixed.get(name, slice(None)) for name in "baz") + (slice(None), c)
 
         landing = ((r1, r2, r3)[step])[part].at[n]
         copy = remote(
-            acc.at[block({**kept, axis: 1 - place[axis]})],
+            acc[part].at[block({**kept, axis: 1 - place[axis]})],
             landing,
             h_r.at[n, part, step],
             {"sample": other[axis]},
         )
         return copy, block({**kept, axis: place[axis]}), landing
 
-    def across(n):
-        core_copy(n).wait_recv()
-        acc[n, :, :, :, :, c] += rc[n]
-        for part in range(3):
-            halving(n, part, 0)[0].start()
-
-    def onward(n, step):
-        for part in range(3):
+    def advance(n, part, step):
+        if step < 0:
+            core_copy(n, part).wait_recv()
+            acc[part][n, :, :, :, :, c] += rc[part][n]
+        else:
             copy, kept, landing = halving(n, part, step)
             copy.wait_recv()
-            acc[kept] += landing[...]
-            halving(n, part, step + 1)[0].start()
+            acc[part][kept] += landing[...]
+        halving(n, part, step + 1)[0].start()
 
     def tile_copy(d):
         return remote(tsrc.at[(s + d) % N_SAMPLE], trcv.at[d], t_r, sample_of(d))
@@ -325,75 +352,76 @@
         tiles = [jnp.where(spot < 64, pltpu.roll(own[2 * i], 64, 1), own[2 * i + 1]) for i in range(n_tiles)]
         m_sc[...] = solve(factor, jnp.concatenate(tiles, axis=1))
 
-    def finish(n):
+    def finish(n, part):
         corr = corr_sc[0:8, :]
         coef = m_sc[:, n * n_cols : (n + 1) * n_cols]
+        copy, kept, landing = halving(n, part, 2)
+        copy.wait_recv()
+        value = acc[part][kept] + landing[...]
+        for k in range(*PARTS[part]):
+            out = value[k - PARTS[part][0]]
+            for j in range(types):
+                out = out - corr[:, 8 * k + j : 8 * k + j + 1] * coef[j : j + 1, :]
+            out = out * scale
+            for i in range(per_chunk):
+                mix[n * per_chunk + i, pl.ds(k, 8, stride=types), :] = out[:, 128 * i : 128 * i + 128]
+
+    design(0)
+
+    def own(n, carry):
         for part in range(3):
-            copy, kept, landing = halving(n, part, 2)
-            copy.wait_recv()
-            value = acc[kept] + landing[...]
-            for k in range(*PARTS[part]):
-                out = value[k - PARTS[part][0]]
-                for j in range(types):
-                    out = out - corr[:, 8 * k + j : 8 * k + j + 1] * coef[j : j + 1, :]
-                out = out * scale
-                for i in range(per_chunk):
-                    mix[n * per_chunk + i, pl.ds(k, 8, stride=types), :] = out[:, 128 * i : 128 * i + 128]
-        for i in range(n * per_chunk, (n + 1) * per_chunk):
-            inter_ref[:, 128 * i : 128 * i + 128] = mix[i]
-
-    design(0)
-
-    def own(n, carry):
-        term(n, True)
+            term(n, part, True)
         return carry
 
     lax.fori_loop(0, N_CHUNK, own, 0)
+    small_term(0)
     for d in (1, 3, 2):
         props_copy(d).wait_recv()
         design(d)
 
     def others(n, carry):
-        term(n, False)
-        small_term(n)
-        core_copy(n).start()
-
-        @pl.when(n == N_CHUNK - 1)
-        def _():
-            send_tiles()
-
-        for chunk in range(1, N_CHUNK):
-            @pl.when(n == chunk)
-            def _(chunk=chunk):
-                across(chunk - 1)
+        for part in range(3):
+            term(n, part, False)
+            core_copy(n, part).start()
+            if part == 2:
+                @pl.when(n > 0)
+                def _():
+                    small_term(n)
+
+            for chunk in range(N_CHUNK):
+                events = DURING.get((chunk, part), ())
+                if events:
+                    @pl.when(n == chunk)
+                    def _(events=events):
+                        for event in events:
+                            advance(*event)
 
         return carry
 
     lax.fori_loop(0, N_CHUNK, others, 0)
-
-    onward(0, 0)
-    across(3)
-    onward(1, 0)
-    spread_tiles()
-    onward(0, 1)
-    onward(2, 0)
-    onward(3, 0)
-    onward(1, 1)
-    onward(2, 1)
+    send_tiles()
+    for event in AFTER:
+        if event == "spread":
+            spread_tiles()
+        else:
+            advance(*event)
     solve_coef()
-    finish(0)
-    onward(3, 1)
-    finish(1)
-    finish(2)
-    finish(3)
+    left = [3] * N_CHUNK
+    for n, part in LAST:
+        finish(n, part)
+        left[n] -= 1
+        if left[n] == 0:
+            for i in range(n * per_chunk, (n + 1) * per_chunk):
+                inter_ref[:, 128 * i : 128 * i + 128] = mix[i]
 
     for d in range(1, N_GENE):
         gram_copy(d).wait_send()
-        rhs_copy(d).wait_send()
+        for h in range(2):
+            rhs_copy(d, h).wait_send()
         props_copy(d).wait_send()
     for n in range(N_CHUNK):
-        core_copy(n).wait_send()
         for part in range(3):
+            core_copy(n, part).wait_send()
             for step in range(3):
                 halving(n, part, step)[0].wait_send()
 
@@ -403,6 +431,17 @@
         return carry
 
     lax.fori_loop(1, N_SAMPLE, drain_tiles, 0)
+
+
+def store(inter_ref, props_ref, inter_out, props_out, sem):
+    copies = (
+        pltpu.make_async_copy(inter_ref, inter_out, sem.at[0]),
+        pltpu.make_async_copy(props_ref, props_out, sem.at[1]),
+    )
+    for copy in copies:
+        copy.start()
+    for copy in copies:
+        copy.wait()
 
 
 def local(expression, profile, dosage, signature):
@@ -436,14 +475,14 @@
             vmem((types, g_dev), F32),
             vmem((1, sig_cols), jnp.int32),
             vmem((8, g_dev), F32),
-            vmem((N_CHUNK, 2, 2, 2, types, 2, 8, n_cols), F32),
-            vmem((N_CHUNK, 2, 2, 2, types, 8, n_cols), F32),
+            [vmem((N_CHUNK, 2, 2, 2, k, 2, 8, n_cols), F32) for k in sizes],
+            [vmem((N_CHUNK, 2, 2, 2, k, 8, n_cols), F32) for k in sizes],
             [vmem((N_CHUNK, 2, 2, k, 8, n_cols), F32) for k in sizes],
             [vmem((N_CHUNK, 2, k, 8, n_cols), F32) for k in sizes],
             [vmem((N_CHUNK, k, 8, n_cols), F32) for k in sizes],
             vmem((N_GENE, 8, quarter), F32),
-            vmem((N_GENE, 8, quarter), F32),
-            vmem((N_GENE - 1, 8, quarter), F32),
+            vmem((N_GENE, 2, 8, quarter // 2), F32),
+            vmem((N_GENE - 1, 2, 8, quarter // 2), F32),
             vmem((8, 128), F32),
             vmem((N_GENE - 1, 8, 128), F32),
             vmem((v_dev, 128), F32),
@@ -459,9 +498,9 @@
             dma((2,)),
             dma,
             dma((N_GENE - 1,)),
+            dma((N_GENE - 1, 2)),
             dma((N_GENE - 1,)),
-            dma((N_GENE - 1,)),
-            dma((N_CHUNK,)),
+            dma((N_CHUNK, 3)),
             dma((N_CHUNK, 3, 3)),
             dma,
             dma,
@@ -471,6 +510,18 @@
         ),
         name="eqtl",
     )(signature.reshape(1, -1), profile.T, expression, dosage)
+    inter, props_t = pl.pallas_call(
+        store,
+        out_shape=(
+            jax.ShapeDtypeStruct(inter.shape, F32),
+            jax.ShapeDtypeStruct(props_t.shape, F32),
+        ),
+        in_specs=[pl.BlockSpec(memory_space=pltpu.VMEM)] * 2,
+        out_specs=(pl.BlockSpec(memory_space=pl.ANY), pl.BlockSpec(memory_space=pl.ANY)),
+        scratch_shapes=[dma((2,))],
+        compiler_params=pltpu.CompilerParams(vmem_limit_bytes=8 * 1024 * 1024),
+        name="store",
+    )(inter, props_t)
     return inter, props_t.T
 
 

time: 39.6 us -> 42.3 us (1.068)
  Pallas kernels: 37.5 us -> 41.5 us
  local copies, waits for them, and re-layouts: 1.35 us -> 0 us
    pallas_call x1, Pallas kernels: 37.5 us -> 40.8 us  [local(): pl.pallas_call(functools.partial(kernel, scale), out_shape=(vmem((v_dev *...]
    unnamed x2 -> x0, local copies, waits for them, and re-layouts: 1.35 us -> none
    pallas_call x0 -> x1, Pallas kernels: none -> 0.75 us  [local(): pl.pallas_call(store, out_shape=(jax.ShapeDtypeStruct(inter.shape, F32),...]
where the time goes in v5:
time: 42.3 us; the launch traced here: 42.2 us
  Pallas kernels  41.5 us (98%)
  between operations  0.64 us (2%)
    pallas_call x1, Pallas kernels, local(): pl.pallas_call(functools.partial(kernel, scale), out_shape=(vmem((v_dev *...  40.8 us

profile of v5, /device:TPU:64, one launch (start us, length us, event | category | flops | bytes accessed | tf_op | source)
XLA Modules:
  0.0 42.2 jit_solution(10894480203207401926)
XLA Ops:
  0.6 40.8 %eqtl.1 = (f32[56,1024]{1,0:T(8,128)S(1)}, f32[7,4096]{1,0:T(8,128)S(1)}) custom-call(s32[1,500]{1,0:T(1,128)} %bitcast.4, f32[7,1024]{1,0:T(8,128)} %bitcast.3, bf16[4096,1024]{1,0:T(8,128)(2,1)} %expr_hbm.1, s32[4096,128]{1,0:T(8,128)} %dos_hbm.1), custom_call_target="tpu_custom_call" | custom-call | tf_op jit(solution)/shard_map/eqtl/pallas_call | solution.py:456
  41.4 0.8 %store.1 = (f32[56,1024]{1,0:T(8,128)}, f32[7,4096]{1,0:T(8,128)}) custom-call(f32[56,1024]{1,0:T(8,128)S(1)} %get-tuple-element.6.inter_ref, f32[7,4096]{1,0:T(8,128)S(1)} %get-tuple-element.7.props_ref), custom_call_target="tpu_custom_call" | custom-call | tf_op jit(solution)/shard_map/store/pallas_call | solution.py:513

commit v6 on v5

--- a/solution.py
+++ b/solution.py
@@ -18,27 +18,18 @@
 VMEM_BYTES = 62_000_000
 PARTS = ((0, 2), (2, 4), (4, 7))
 ORDERS = (
-    ("abz", "zab", "baz"),
-    ("azb", "zab", "zab"),
-    ("bza", "abz", "abz"),
-    ("zba", "zab", "bza"),
+    ("bza", "zba", "baz"),
+    ("abz", "zba", "zab"),
+    ("azb", "baz", "bza"),
+    ("abz", "azb", "zba"),
 )
-DURING = {
-    (1, 0): ((0, 0, -1),),
-    (1, 1): ((0, 1, -1),),
-    (1, 2): ((0, 2, -1), (1, 0, -1)),
-    (2, 0): ((1, 1, -1),),
-    (2, 2): ((1, 2, -1), (0, 0, 0), (2, 0, -1), (0, 1, 0)),
-    (3, 0): ((2, 1, -1),),
-    (3, 1): ((1, 0, 0),),
-}
 AFTER = (
-    (2, 2, -1), (1, 1, 0), (0, 2, 0), (3, 0, -1), (3, 1, -1), (0, 0, 1), (0, 1, 1), (3, 2, -1), (1, 2, 0), (2, 0, 0),
-    (2, 1, 0), (1, 0, 1), (3, 0, 0), (2, 2, 0), (3, 2, 0), (1, 1, 1), (3, 1, 0), "spread", (2, 1, 1), (0, 2, 1),
-    (2, 0, 1), (3, 0, 1), (1, 2, 1), (3, 2, 1), (2, 2, 1), (3, 1, 1),
+    (0, 0, 0), (0, 1, 0), (1, 0, 0), (1, 1, 0), (3, 0, -1), (3, 1, -1), (0, 2, 0), (3, 2, -1), (0, 1, 1), (2, 0, 0),
+    (1, 2, 0), (2, 1, 0), "spread", (0, 0, 1), (3, 0, 0), (2, 2, 0), (3, 1, 0), (1, 0, 1), (3, 2, 0), (0, 2, 1),
+    (1, 1, 1), (2, 0, 1), (3, 0, 1), (2, 2, 1), (1, 2, 1), (3, 1, 1), (3, 2, 1), (2, 1, 1),
 )
 LAST = (
-    (0, 0), (0, 1), (1, 0), (0, 2), (2, 1), (1, 1), (2, 0), (1, 2), (3, 0), (3, 2), (2, 2), (3, 1),
+    (1, 0), (2, 0), (0, 0), (0, 1), (1, 1), (0, 2), (3, 0), (2, 2), (1, 2), (3, 1), (2, 1), (3, 2),
 )
 
 
@@ -169,16 +160,18 @@
     def gram_copy(d):
         return remote(gsnd, grcv.at[d - 1], g_r.at[d - 1], gene_of(d))
 
-    def rhs_copy(d, h):
-        return remote(rsnd.at[d, h], rrcv.at[d - 1, h], x_r.at[d - 1, h], gene_of(d))
-
-    def rhs_half(i, carry):
-        d, h = N_GENE - 1 - i // 2, i % 2
+    def rhs_copy(d):
+        return remote(rsnd.at[d], rrcv.at[d - 1], x_r.at[d - 1], gene_of(d))
+
+    def rhs_quarter(i, carry):
+        d = N_GENE - 1 - i
         at = (N_GENE - d) % N_GENE
-        load(at, h).wait()
-        rows = pl.ds(pl.multiple_of(at * quarter + h * half, half), half)
-        part = lax.dot_general(m3, e_v[rows, :], NT, preferred_element_type=F32)
-        rsnd[d, h] = part[0:8] + part[8:16] + part[16:24]
+        for h in range(2):
+            load(at, h).wait()
+        for h in range(2):
+            rows = pl.ds(pl.multiple_of(at * quarter + h * half, half), half)
+            part = lax.dot_general(m3, e_v[rows, :], NT, preferred_element_type=F32)
+            rsnd[d, :, h * half : (h + 1) * half] = part[0:8] + part[8:16] + part[16:24]
 
         @pl.when(i == 0)
         def _():
@@ -188,11 +181,11 @@
 
         @pl.when(d > 0)
         def _():
-            rhs_copy(d, h).start()
+            rhs_copy(d).start()
 
         return carry
 
-    lax.fori_loop(0, 2 * N_GENE, rhs_half, 0)
+    lax.fori_loop(0, N_GENE, rhs_quarter, 0)
 
     for d in range(N_GENE):
         load_dosage(d).wait()
@@ -207,10 +200,8 @@
         gram = gram + grcv[d - 1, :, 0:8]
     factor = ldl(gram)
     for d in (3, 2, 1):
-        for h in range(2):
-            rhs_copy(d, h).wait_recv()
-    for h in range(2):
-        pbuf[g, :, h * half : (h + 1) * half] = solve(factor, rsnd[0, h] + rrcv[2, h] + rrcv[1, h] + rrcv[0, h])
+        rhs_copy(d).wait_recv()
+    pbuf[g] = solve(factor, rsnd[0] + rrcv[2] + rrcv[1] + rrcv[0])
 
     def props_copy(d):
         return remote(pbuf.at[g], pbuf.at[g], p_r.at[d - 1], gene_of(d))
@@ -253,19 +244,15 @@
         corr_sc[:, 0 : 16 * types] += corr
         pp_sc[:, 0:16] += pp[0:8] + pp[8:16]
 
-    def term(n, part, first):
+    def term(n, first):
         columns = pl.ds(pl.multiple_of(n * n_cols, n_cols), n_cols)
         span = slice(0, quarter) if first else slice(quarter, s_dev)
-        lo, hi = PARTS[part]
-        size = 128 * (hi - lo)
-        last = part == len(PARTS) - 1
-        rows = slice(128 * lo, 128 * hi + (16 if last else 0))
-        value = jnp.dot(des[rows, span], e_v[span, columns], preferred_element_type=F32)
-        body = value[0:size].reshape(acc[part].shape[1:])
-        acc[part][n] = body if first else acc[part][n] + body
-        if last:
-            tail = value[size : size + 8] + value[size + 8 : size + 16]
-            py_sc[n] = tail if first else py_sc[n] + tail
+        value = jnp.dot(des[:, span], e_v[span, columns], preferred_element_type=F32)
+        for part, (lo, hi) in enumerate(PARTS):
+            body = value[128 * lo : 128 * hi].reshape(acc[part].shape[1:])
+            acc[part][n] = body if first else acc[part][n] + body
+        tail = value[896:904] + value[904:912]
+        py_sc[n] = tail if first else py_sc[n] + tail
 
     def core_copy(n, part):
         return remote(
@@ -369,8 +356,7 @@
     design(0)
 
     def own(n, carry):
-        for part in range(3):
-            term(n, part, True)
+        term(n, True)
         return carry
 
     lax.fori_loop(0, N_CHUNK, own, 0)
@@ -380,26 +366,27 @@
         design(d)
 
     def others(n, carry):
+        term(n, False)
         for part in range(3):
-            term(n, part, False)
             core_copy(n, part).start()
-            if part == 2:
-                @pl.when(n > 0)
-                def _():
-                    small_term(n)
-
-            for chunk in range(N_CHUNK):
-                events = DURING.get((chunk, part), ())
-                if events:
-                    @pl.when(n == chunk)
-                    def _(events=events):
-                        for event in events:
-                            advance(*event)
+
+        @pl.when(n > 0)
+        def _():
+            small_term(n)
+
+        @pl.when(n == N_CHUNK - 1)
+        def _():
+            send_tiles()
+
+        for chunk in range(1, N_CHUNK):
+            @pl.when(n == chunk)
+            def _(chunk=chunk):
+                for part in range(3):
+                    advance(chunk - 1, part, -1)
 
         return carry
 
     lax.fori_loop(0, N_CHUNK, others, 0)
-    send_tiles()
     for event in AFTER:
         if event == "spread":
             spread_tiles()
@@ -416,8 +403,7 @@
 
     for d in range(1, N_GENE):
         gram_copy(d).wait_send()
-        for h in range(2):
-            rhs_copy(d, h).wait_send()
+        rhs_copy(d).wait_send()
         props_copy(d).wait_send()
     for n in range(N_CHUNK):
         for part in range(3):
@@ -481,8 +467,8 @@
             [vmem((N_CHUNK, 2, k, 8, n_cols), F32) for k in sizes],
             [vmem((N_CHUNK, k, 8, n_cols), F32) for k in sizes],
             vmem((N_GENE, 8, quarter), F32),
-            vmem((N_GENE, 2, 8, quarter // 2), F32),
-            vmem((N_GENE - 1, 2, 8, quarter // 2), F32),
+            vmem((N_GENE, 8, quarter), F32),
+            vmem((N_GENE - 1, 8, quarter), F32),
             vmem((8, 128), F32),
             vmem((N_GENE - 1, 8, 128), F32),
             vmem((v_dev, 128), F32),
@@ -498,7 +484,7 @@
             dma((2,)),
             dma,
             dma((N_GENE - 1,)),
-            dma((N_GENE - 1, 2)),
+            dma((N_GENE - 1,)),
             dma((N_GENE - 1,)),
             dma((N_CHUNK, 3)),
             dma((N_CHUNK, 3, 3)),

time: 42.3 us -> 40.5 us (0.957)
  Pallas kernels: 41.5 us -> 39.7 us
    pallas_call x1, Pallas kernels: 40.8 us -> 38.9 us  [local(): pl.pallas_call(functools.partial(kernel, scale), out_shape=(vmem((v_dev *...]
where the time goes in v6:
time: 40.5 us; the launch traced here: 40.3 us
  Pallas kernels  39.7 us (98%)
  between operations  0.64 us (2%)
    pallas_call x1, Pallas kernels, local(): pl.pallas_call(functools.partial(kernel, scale), out_shape=(vmem((v_dev *...  38.9 us

profile of v6, /device:TPU:64, one launch (start us, length us, event | category | flops | bytes accessed | tf_op | source)
XLA Modules:
  0.0 40.3 jit_solution(3218771080712090667)
XLA Ops:
  0.6 38.9 %eqtl.1 = (f32[56,1024]{1,0:T(8,128)S(1)}, f32[7,4096]{1,0:T(8,128)S(1)}) custom-call(s32[1,500]{1,0:T(1,128)} %bitcast.4, f32[7,1024]{1,0:T(8,128)} %bitcast.3, bf16[4096,1024]{1,0:T(8,128)(2,1)} %expr_hbm.1, s32[4096,128]{1,0:T(8,128)} %dos_hbm.1), custom_call_target="tpu_custom_call" | custom-call | tf_op jit(solution)/shard_map/eqtl/pallas_call | solution.py:442
  39.6 0.8 %store.1 = (f32[56,1024]{1,0:T(8,128)}, f32[7,4096]{1,0:T(8,128)}) custom-call(f32[56,1024]{1,0:T(8,128)S(1)} %get-tuple-element.6.inter_ref, f32[7,4096]{1,0:T(8,128)S(1)} %get-tuple-element.7.props_ref), custom_call_target="tpu_custom_call" | custom-call | tf_op jit(solution)/shard_map/store/pallas_call | solution.py:499

commit v7 on v6

--- a/solution.py
+++ b/solution.py
@@ -18,18 +18,18 @@
 VMEM_BYTES = 62_000_000
 PARTS = ((0, 2), (2, 4), (4, 7))
 ORDERS = (
-    ("bza", "zba", "baz"),
-    ("abz", "zba", "zab"),
-    ("azb", "baz", "bza"),
-    ("abz", "azb", "zba"),
+    ("azb", "baz", "zba"),
+    ("abz", "zba", "bza"),
+    ("azb", "baz", "baz"),
+    ("zab", "zba", "azb"),
 )
 AFTER = (
-    (0, 0, 0), (0, 1, 0), (1, 0, 0), (1, 1, 0), (3, 0, -1), (3, 1, -1), (0, 2, 0), (3, 2, -1), (0, 1, 1), (2, 0, 0),
-    (1, 2, 0), (2, 1, 0), "spread", (0, 0, 1), (3, 0, 0), (2, 2, 0), (3, 1, 0), (1, 0, 1), (3, 2, 0), (0, 2, 1),
-    (1, 1, 1), (2, 0, 1), (3, 0, 1), (2, 2, 1), (1, 2, 1), (3, 1, 1), (3, 2, 1), (2, 1, 1),
+    (0, 2, 0), (3, 0, -1), (1, 0, 0), (3, 1, -1), (1, 1, 0), (3, 2, -1), (1, 2, 0), (0, 0, 1), (0, 1, 1), "spread",
+    (2, 1, 0), (2, 0, 0), (3, 0, 0), (2, 2, 0), (3, 1, 0), (3, 2, 0), (0, 2, 1), (1, 2, 1), (1, 0, 1), (2, 1, 1),
+    (1, 1, 1), (3, 0, 1), (2, 0, 1), (2, 2, 1), (3, 2, 1), (3, 1, 1),
 )
 LAST = (
-    (1, 0), (2, 0), (0, 0), (0, 1), (1, 1), (0, 2), (3, 0), (2, 2), (1, 2), (3, 1), (2, 1), (3, 2),
+    (0, 1), (0, 0), (1, 0), (0, 2), (2, 1), (1, 2), (3, 0), (1, 1), (2, 0), (2, 2), (3, 2), (3, 1),
 )
 
 
@@ -381,6 +381,9 @@
         for chunk in range(1, N_CHUNK):
             @pl.when(n == chunk)
             def _(chunk=chunk):
+                if chunk == N_CHUNK - 1:
+                    advance(0, 0, 0)
+                    advance(0, 1, 0)
                 for part in range(3):
                     advance(chunk - 1, part, -1)
 

time: 40.5 us -> 38.8 us (0.958)
  Pallas kernels: 39.7 us -> 38 us
    pallas_call x1, Pallas kernels: 38.9 us -> 37.3 us  [local(): pl.pallas_call(functools.partial(kernel, scale), out_shape=(vmem((v_dev *...]
where the time goes in v7:
time: 38.8 us; the launch traced here: 38.7 us
  Pallas kernels  38 us (98%)
  between operations  0.64 us (2%)
    pallas_call x1, Pallas kernels, local(): pl.pallas_call(functools.partial(kernel, scale), out_shape=(vmem((v_dev *...  37.3 us

profile of v7, /device:TPU:64, one launch (start us, length us, event | category | flops | bytes accessed | tf_op | source)
XLA Modules:
  0.0 38.7 jit_solution(16629862559417532176)
XLA Ops:
  0.6 37.3 %eqtl.1 = (f32[56,1024]{1,0:T(8,128)S(1)}, f32[7,4096]{1,0:T(8,128)S(1)}) custom-call(s32[1,500]{1,0:T(1,128)} %bitcast.4, f32[7,1024]{1,0:T(8,128)} %bitcast.3, bf16[4096,1024]{1,0:T(8,128)(2,1)} %expr_hbm.1, s32[4096,128]{1,0:T(8,128)} %dos_hbm.1), custom_call_target="tpu_custom_call" | custom-call | tf_op jit(solution)/shard_map/eqtl/pallas_call | solution.py:445
  37.9 0.8 %store.1 = (f32[56,1024]{1,0:T(8,128)}, f32[7,4096]{1,0:T(8,128)}) custom-call(f32[56,1024]{1,0:T(8,128)S(1)} %get-tuple-element.6.inter_ref, f32[7,4096]{1,0:T(8,128)S(1)} %get-tuple-element.7.props_ref), custom_call_target="tpu_custom_call" | custom-call | tf_op jit(solution)/shard_map/store/pallas_call | solution.py:502

commit v8 on v7

--- a/solution.py
+++ b/solution.py
@@ -24,7 +24,7 @@
     ("zab", "zba", "azb"),
 )
 AFTER = (
-    (0, 2, 0), (3, 0, -1), (1, 0, 0), (3, 1, -1), (1, 1, 0), (3, 2, -1), (1, 2, 0), (0, 0, 1), (0, 1, 1), "spread",
+    (0, 2, 0), "small", (3, 0, -1), (1, 0, 0), (3, 1, -1), (1, 1, 0), (3, 2, -1), (1, 2, 0), (0, 0, 1), (0, 1, 1), "spread",
     (2, 1, 0), (2, 0, 0), (3, 0, 0), (2, 2, 0), (3, 1, 0), (3, 2, 0), (0, 2, 1), (1, 2, 1), (1, 0, 1), (2, 1, 1),
     (1, 1, 1), (3, 0, 1), (2, 0, 1), (2, 2, 1), (3, 2, 1), (3, 1, 1),
 )
@@ -117,14 +117,14 @@
     prof_copy = pltpu.make_async_copy(prof_hbm, prof_ref, i_sem.at[1])
     sig_copy.start()
     prof_copy.start()
-    for h in range(2):
-        load(1, h).start()
-
     barrier = pltpu.get_barrier_semaphore()
     for d in range(1, N_GENE):
         pl.semaphore_signal(barrier, inc=1, device_id=gene_of(d), device_id_type=MESH)
     for d in range(1, N_SAMPLE):
         pl.semaphore_signal(barrier, inc=1, device_id=sample_of(d), device_id_type=MESH)
+
+    for h in range(2):
+        load(1, h).start()
 
     n_sig = sig_ref.shape[1]
     sig_sc[...] = jnp.full(sig_sc.shape, -1, jnp.int32)
@@ -370,14 +370,6 @@
         for part in range(3):
             core_copy(n, part).start()
 
-        @pl.when(n > 0)
-        def _():
-            small_term(n)
-
-        @pl.when(n == N_CHUNK - 1)
-        def _():
-            send_tiles()
-
         for chunk in range(1, N_CHUNK):
             @pl.when(n == chunk)
             def _(chunk=chunk):
@@ -390,8 +382,16 @@
         return carry
 
     lax.fori_loop(0, N_CHUNK, others, 0)
+
+    def small_more(d, carry):
+        small_term(d)
+        return carry
+
     for event in AFTER:
-        if event == "spread":
+        if event == "small":
+            lax.fori_loop(1, N_GENE, small_more, 0)
+            send_tiles()
+        elif event == "spread":
             spread_tiles()
         else:
             advance(*event)

time: 38.8 us -> 41 us (1.057)
  Pallas kernels: 38 us -> 40.2 us
    pallas_call x1, Pallas kernels: 37.3 us -> 39.5 us  [local(): pl.pallas_call(functools.partial(kernel, scale), out_shape=(vmem((v_dev *...]
where the time goes in v8:
time: 41 us; the launch traced here: 40.9 us
  Pallas kernels  40.2 us (98%)
  between operations  0.64 us (2%)
    pallas_call x1, Pallas kernels, local(): pl.pallas_call(functools.partial(kernel, scale), out_shape=(vmem((v_dev *...  39.5 us

profile of v8, /device:TPU:64, one launch (start us, length us, event | category | flops | bytes accessed | tf_op | source)
XLA Modules:
  0.0 40.9 jit_solution(15264874636882233348)
XLA Ops:
  0.6 39.5 %eqtl.1 = (f32[56,1024]{1,0:T(8,128)S(1)}, f32[7,4096]{1,0:T(8,128)S(1)}) custom-call(s32[1,500]{1,0:T(1,128)} %bitcast.4, f32[7,1024]{1,0:T(8,128)} %bitcast.3, bf16[4096,1024]{1,0:T(8,128)(2,1)} %expr_hbm.1, s32[4096,128]{1,0:T(8,128)} %dos_hbm.1), custom_call_target="tpu_custom_call" | custom-call | tf_op jit(solution)/shard_map/eqtl/pallas_call | solution.py:445
  40.1 0.8 %store.1 = (f32[56,1024]{1,0:T(8,128)}, f32[7,4096]{1,0:T(8,128)}) custom-call(f32[56,1024]{1,0:T(8,128)S(1)} %get-tuple-element.6.inter_ref, f32[7,4096]{1,0:T(8,128)S(1)} %get-tuple-element.7.props_ref), custom_call_target="tpu_custom_call" | custom-call | tf_op jit(solution)/shard_map/store/pallas_call | solution.py:502

commit v9 on v7

--- a/solution.py
+++ b/solution.py
@@ -25,7 +25,7 @@
 )
 AFTER = (
     (0, 2, 0), (3, 0, -1), (1, 0, 0), (3, 1, -1), (1, 1, 0), (3, 2, -1), (1, 2, 0), (0, 0, 1), (0, 1, 1), "spread",
-    (2, 1, 0), (2, 0, 0), (3, 0, 0), (2, 2, 0), (3, 1, 0), (3, 2, 0), (0, 2, 1), (1, 2, 1), (1, 0, 1), (2, 1, 1),
+    (2, 1, 0), (2, 0, 0), (3, 0, 0), "factor", (2, 2, 0), (3, 1, 0), (3, 2, 0), (0, 2, 1), (1, 2, 1), (1, 0, 1), (2, 1, 1),
     (1, 1, 1), (3, 0, 1), (2, 0, 1), (2, 2, 1), (3, 2, 1), (3, 1, 1),
 )
 LAST = (
@@ -327,6 +327,9 @@
         tbuf[0] = total
         lax.fori_loop(1, N_SAMPLE, start_spread, 0)
         corr_sc[0:8, :] = total
+
+    def factor_pp():
+        total = corr_sc[0:8, :]
         inv, inv_t, diag = ldl(pltpu.roll(total, 128 - n_kj, 1)[:, 0:8])
         fac_sc[0, :, 0:8] = inv
         fac_sc[1, :, 0:8] = inv_t
@@ -376,14 +379,13 @@
 
         @pl.when(n == N_CHUNK - 1)
         def _():
+            advance(0, 0, 0)
+            advance(0, 1, 0)
             send_tiles()
 
         for chunk in range(1, N_CHUNK):
             @pl.when(n == chunk)
             def _(chunk=chunk):
-                if chunk == N_CHUNK - 1:
-                    advance(0, 0, 0)
-                    advance(0, 1, 0)
                 for part in range(3):
                     advance(chunk - 1, part, -1)
 
@@ -393,6 +395,8 @@
     for event in AFTER:
         if event == "spread":
             spread_tiles()
+        elif event == "factor":
+            factor_pp()
         else:
             advance(*event)
     solve_coef()

time: 38.8 us -> 38.9 us (level)
  no operation moved by 1% of the time
where the time goes in v9:
time: 38.9 us; the launch traced here: 38.8 us
  Pallas kernels  38.2 us (98%)
  between operations  0.64 us (2%)
    pallas_call x1, Pallas kernels, local(): pl.pallas_call(functools.partial(kernel, scale), out_shape=(vmem((v_dev *...  37.4 us

profile of v9, /device:TPU:64, one launch (start us, length us, event | category | flops | bytes accessed | tf_op | source)
XLA Modules:
  0.0 38.8 jit_solution(6749865086043898850)
XLA Ops:
  0.6 37.4 %eqtl.1 = (f32[56,1024]{1,0:T(8,128)S(1)}, f32[7,4096]{1,0:T(8,128)S(1)}) custom-call(s32[1,500]{1,0:T(1,128)} %bitcast.4, f32[7,1024]{1,0:T(8,128)} %bitcast.3, bf16[4096,1024]{1,0:T(8,128)(2,1)} %expr_hbm.1, s32[4096,128]{1,0:T(8,128)} %dos_hbm.1), custom_call_target="tpu_custom_call" | custom-call | tf_op jit(solution)/shard_map/eqtl/pallas_call | solution.py:449
  38.1 0.8 %store.1 = (f32[56,1024]{1,0:T(8,128)}, f32[7,4096]{1,0:T(8,128)}) custom-call(f32[56,1024]{1,0:T(8,128)S(1)} %get-tuple-element.6.inter_ref, f32[7,4096]{1,0:T(8,128)S(1)} %get-tuple-element.7.props_ref), custom_call_target="tpu_custom_call" | custom-call | tf_op jit(solution)/shard_map/store/pallas_call | solution.py:506
